TPU v7x, 32 devices: a whole 2x2x4 slice. The times are simulated.
32 devices in a mesh: lon: 8 (over z, x), lat: 4 (over y, core).
Axes of the slice: x: 2, y: 2, z: 4, core: 2. Of those that a mesh axis runs over, the one named last changes fastest.
Arguments:
- expanded: bfloat16 [32, 128, 3072], P('lat', 'lon'), may hold values from -6 to 6
- stream: bfloat16 [32, 128, 768], P('lat', 'lon'), may hold values from -6 to 6
- land: int32 [32, 128], P('lat', 'lon'), may hold values 0 or 1
- polar: int32 [32], replicated, may hold values from 0 to 1, as said below
- land_shift: float32 [3072], replicated, may hold values from -4 to 4
- dw_kernel: float32 [3, 3, 3072], replicated, may hold values from -2 to 2
- w_proj: bfloat16 [3072, 768], replicated, may hold values from -0.109375 to 0.109375
- w_qkv: bfloat16 [768, 2304], replicated, may hold values from -0.21875 to 0.21875
- w_out: bfloat16 [768, 768], replicated, may hold values from -0.21875 to 0.21875
- rel_bias: float32 [24, 15, 8], replicated, may hold values from -2 to 250
Outputs:
- mixed_out: bfloat16 [32, 128, 768], P('lat', 'lon')
Inputs may be any that keep to these rules, and one draw needn't show every extreme that they name: `polar`: 1 marks the first a and the last b token rows, 1 <= a, b <= 4, at least one of a, b equal to 4; all other rows are 0.
All inputs are finite; a program needn't handle non-finite values. No bound on the sum of `land` on one device may be relied on, other than what follows from the above.
Results may differ from a plain program's by a relative error of at most 0.0075.
Values may be sent and summed in bfloat16 or wider, within the bound.
A program may use at most 128 MiB of HBM per device.

v0:
```python
import jax
import jax.numpy as jnp
from jax import lax
from jax.sharding import PartitionSpec as P

GRID = 8


eps = 1e-05


def padded(cells, sides, width, closed):
    for axis, dim in sides:
        count = lax.axis_size(axis)
        ends = count if closed else count - 1
        head = lax.slice_in_dim(cells, 0, width, axis=dim)
        tail = lax.slice_in_dim(cells, cells.shape[dim] - width, cells.shape[dim], axis=dim)
        cells = jnp.concatenate(
            [
                lax.ppermute(tail, axis, [(i, (i + 1) % count) for i in range(ends)]),
                cells,
                lax.ppermute(head, axis, [((i + 1) % count, i) for i in range(ends)]),
            ],
            axis=dim,
        )
    return cells


def shifted(x, axis, by):
    peers = lax.axis_size(axis)
    return lax.ppermute(x, axis, [(i, (i + by) % peers) for i in range(peers)])


def spread_bias(table_hop):
    query_pos = jnp.arange(GRID)[:, None]
    key_pos = jnp.arange(GRID)[None, :]
    offsets = key_pos - query_pos + GRID - 1
    choose = (offsets[:, :, None] == jnp.arange(2 * GRID - 1)[None, None, :]).astype(jnp.float32)
    return jnp.einsum("hs,mks->hmk", table_hop, choose)


def absorb(state, queries, keys, values, bias, key_ok, factor_scale):
    peak, total, summed = state
    scores = (
        jnp.einsum("mghd,kghd->ghmk", queries, keys, preferred_element_type=jnp.float32)
        * factor_scale
        + bias[None]
    )
    scores = jnp.where(key_ok[:, None, None, :], scores, -1e30)
    new_peak = jnp.maximum(peak, jnp.max(scores, axis=-1))
    factor = jnp.exp(peak - new_peak)
    weights = jnp.exp(scores - new_peak[..., None])
    total = total * factor + jnp.sum(weights, axis=-1)
    summed = summed * factor[..., None] + jnp.einsum(
        "ghmk,kghd->ghmd", weights.astype(jnp.bfloat16), values, preferred_element_type=jnp.float32
    )
    return (new_peak, total, summed)


def local(expanded, stream, land, polar, land_shift, dw_kernel, w_proj, w_qkv, w_out, rel_bias):
    rows_dev, cols_dev, width_exp = expanded.shape
    width = stream.shape[2]
    heads = rel_bias.shape[0]
    head_dim = width // heads
    extended = padded(expanded, (("lat", 0),), 1, False)
    extended = padded(extended, (("lon", 1),), 1, True)
    filtered = land[:, :, None].astype(jnp.float32) * land_shift[None, None, :]
    for row_tap in range(3):
        for col_tap in range(3):
            filtered = (
                filtered
                + extended[row_tap : row_tap + rows_dev, col_tap : col_tap + cols_dev]
                * dw_kernel[row_tap, col_tap]
            )
    activated = jax.nn.gelu(filtered).astype(jnp.bfloat16)
    projected = jnp.dot(
        activated.reshape(-1, width_exp), w_proj, preferred_element_type=jnp.float32
    )
    mixed = (stream.astype(jnp.float32) + projected.reshape(rows_dev, cols_dev, width)).astype(
        jnp.bfloat16
    )
    columns = lax.all_to_all(mixed, "lat", split_axis=1, concat_axis=0, tiled=True)
    all_rows, col_here = (columns.shape[0], columns.shape[1])
    strip = all_rows // GRID
    groups = strip * col_here
    flat = columns.reshape(-1, width).astype(jnp.float32)
    centre = jnp.mean(flat, axis=1, keepdims=True)
    centred = flat - centre
    spread = jnp.mean(centred * centred, axis=1, keepdims=True)
    normed = (centred * lax.rsqrt(spread + eps)).astype(jnp.bfloat16)

    def heads_view(block):
        return block.reshape(GRID, groups, heads, head_dim)

    queries = heads_view(
        jnp.dot(normed, w_qkv[:, :width], preferred_element_type=jnp.float32).astype(jnp.bfloat16)
    )
    paired = jnp.dot(normed, w_qkv[:, width:], preferred_element_type=jnp.float32).astype(
        jnp.bfloat16
    )
    keys = heads_view(paired[:, :width])
    values = heads_view(paired[:, width:])
    cap_rows = polar.reshape(GRID, strip)
    factor_scale = head_dim ** (-0.5)
    stride = lax.axis_size("lon") // GRID
    key_ok = jnp.repeat(jnp.transpose(cap_rows == 0), col_here, axis=0)
    state = (
        jnp.full((groups, heads, GRID), -1e30, jnp.float32),
        jnp.zeros((groups, heads, GRID), jnp.float32),
        jnp.zeros((groups, heads, GRID, head_dim), jnp.float32),
    )
    state, key_ok = (
        absorb(state, queries, keys, values, spread_bias(rel_bias[:, :, 0]), key_ok, factor_scale),
        key_ok,
    )
    far_keys, far_values = (keys, values)
    for hop in range(1, GRID):
        far_keys, far_values = shifted((far_keys, far_values), "lon", stride)
        state = absorb(
            state,
            queries,
            far_keys,
            far_values,
            spread_bias(rel_bias[:, :, GRID - hop]),
            key_ok,
            factor_scale,
        )
    peak, total, summed = state
    joined = summed / total[..., None]
    attended = jnp.transpose(joined, (2, 0, 1, 3)).reshape(-1, width).astype(jnp.bfloat16)
    result = flat + jnp.dot(attended, w_out, preferred_element_type=jnp.float32)
    result = result.astype(jnp.bfloat16).reshape(all_rows, col_here, width)
    return lax.all_to_all(result, "lat", split_axis=0, concat_axis=1, tiled=True)


def solution(mesh):
    in_specs = (
        P("lat", "lon", None),
        P("lat", "lon", None),
        P("lat", "lon"),
        P(),
        P(),
        P(),
        P(),
        P(),
        P(),
        P(),
    )
    out_specs = P("lat", "lon", None)
    return jax.shard_map(local, mesh=mesh, in_specs=in_specs, out_specs=out_specs, check_vma=False)
```

profile of v0, /device:TPU:0, one launch (start us, length us, event | category | flops | bytes accessed | tf_op | source)
XLA Modules:
  0.0 310.0 jit_solution(7786040148013927238)
XLA Ops:
  1.1 2.4 collective-permute-start
  11.3 2.4 collective-permute-start.2
  13.7 3.1 %collective-permute-start.3 = (bf16[10,1,3072]{2,1,0:T(2,128)(2,1)S(1)}, bf16[10,1,3072]{2,1,0:T(2,128)(2,1)}, u32[]{:S(2)}, u32[]{:S(2)}) collective-permute-start(bf16[10,1,3072]{2,1,0:T(2,128)(2,1)S(1)} %get-tuple-element.22), channel_id=1, source_target_pairs={{4,0},{8,4},{12,8},{16,12},{20,16},{24,20},{28,24},{0,28},{5,1},{9... | collective-permute-start | bytes 184328 | tf_op jit(solution)/shard_map/ppermute | solution.py:22
  27.2 6.3 %fusion.41 = bf16[8,16,768]{2,1,0:T(8,128)(2,1)S(1)} fusion(bf16[3072,768]{1,0:T(8,128)(2,1)} %param.16, bf16[8,16,3072]{2,1,0:T(8,128)(2,1)S(1)} %copy-done.3, bf16[10,16,3072]{2,1,0:T(8,128)(2,1)S(1)} %constant_dynamic-update-slice_fusion, bf16[10,1,3072]{2,1,0:T(2,128)(2,1)} %collective-permute-done.3, bf16[10,1,3072]{2,1,0:T(2,128)(2,1)} %collective-permute-done.2, ...), kind=kOutput, calls=%fused_computation.74 | convolution fusion | flops 628260864 | bytes 7324160 | tf_op jit(solution)/shard_map/dot_general | solution.py:76
  34.2 5.4 %all-to-all-start = ((bf16[8,16,768]{2,0,1:T(8,128)(2,1)}), bf16[8,16,768]{2,0,1:T(8,128)(2,1)S(1)}, u32[]{:S(2)}, u32[]{:S(2)}) async-start(bf16[8,16,768]{2,0,1:T(8,128)(2,1)} %copy.136), calls=%async_computation | async-start | bytes 393216 | tf_op jit(solution)/shard_map/all_to_all | solution.py:82
  40.6 4.4 %all-to-all-done = bf16[8,16,768]{2,0,1:T(8,128)(2,1)S(1)} async-done(((bf16[8,16,768]{2,0,1:T(8,128)(2,1)}), bf16[8,16,768]{2,0,1:T(8,128)(2,1)S(1)}, u32[]{:S(2)}, u32[]{:S(2)}) %all-to-all-start) | async-done | bytes 196640 | tf_op jit(solution)/shard_map/all_to_all | solution.py:82
  48.4 2.2 convolution_convert_fusion
  58.6 18.6 %collective-permute-done.4 = bf16[8,16,24,32]{3,0,2,1:T(8,128)(2,1)} collective-permute-done((bf16[8,16,24,32]{3,0,2,1:T(8,128)(2,1)}, bf16[8,16,24,32]{3,0,2,1:T(8,128)(2,1)}, u32[]{:S(2)}, u32[]{:S(2)}) %collective-permute-start.4) | collective-permute-done | bytes 196640 | tf_op jit(solution)/shard_map/ppermute | solution.py:31
  77.2 16.7 %collective-permute-done.5 = bf16[8,16,24,32]{3,0,2,1:T(8,128)(2,1)S(1)} collective-permute-done((bf16[8,16,24,32]{3,0,2,1:T(8,128)(2,1)S(1)}, bf16[8,16,24,32]{3,0,2,1:T(8,128)(2,1)S(1)}, u32[]{:S(2)}, u32[]{:S(2)}) %collective-permute-start.5) | collective-permute-done | bytes 196640 | tf_op jit(solution)/shard_map/ppermute | solution.py:31
  93.9 2.2 fusion.135
  96.1 14.6 %collective-permute-done.6 = bf16[8,16,24,32]{3,0,2,1:T(8,128)(2,1)S(1)} collective-permute-done((bf16[8,16,24,32]{3,0,2,1:T(8,128)(2,1)}, bf16[8,16,24,32]{3,0,2,1:T(8,128)(2,1)S(1)}, u32[]{:S(2)}, u32[]{:S(2)}) %collective-permute-start.6) | collective-permute-done | bytes 196640 | tf_op jit(solution)/shard_map/ppermute | solution.py:31
  110.8 16.8 %collective-permute-done.7 = bf16[8,16,24,32]{3,0,2,1:T(8,128)(2,1)S(1)} collective-permute-done((bf16[8,16,24,32]{3,0,2,1:T(8,128)(2,1)S(1)}, bf16[8,16,24,32]{3,0,2,1:T(8,128)(2,1)S(1)}, u32[]{:S(2)}, u32[]{:S(2)}) %collective-permute-start.7) | collective-permute-done | bytes 196640 | tf_op jit(solution)/shard_map/ppermute | solution.py:31
  128.7 15.8 %collective-permute-done.8 = bf16[8,16,24,32]{3,0,2,1:T(8,128)(2,1)S(1)} collective-permute-done((bf16[8,16,24,32]{3,0,2,1:T(8,128)(2,1)S(1)}, bf16[8,16,24,32]{3,0,2,1:T(8,128)(2,1)S(1)}, u32[]{:S(2)}, u32[]{:S(2)}) %collective-permute-start.8) | collective-permute-done | bytes 196640 | tf_op jit(solution)/shard_map/ppermute | solution.py:31
  144.5 16.8 %collective-permute-done.9 = bf16[8,16,24,32]{3,0,2,1:T(8,128)(2,1)S(1)} collective-permute-done((bf16[8,16,24,32]{3,0,2,1:T(8,128)(2,1)S(1)}, bf16[8,16,24,32]{3,0,2,1:T(8,128)(2,1)S(1)}, u32[]{:S(2)}, u32[]{:S(2)}) %collective-permute-start.9) | collective-permute-done | bytes 196640 | tf_op jit(solution)/shard_map/ppermute | solution.py:31
  162.4 15.8 %collective-permute-done.10 = bf16[8,16,24,32]{3,0,2,1:T(8,128)(2,1)S(1)} collective-permute-done((bf16[8,16,24,32]{3,0,2,1:T(8,128)(2,1)S(1)}, bf16[8,16,24,32]{3,0,2,1:T(8,128)(2,1)S(1)}, u32[]{:S(2)}, u32[]{:S(2)}) %collective-permute-start.10) | collective-permute-done | bytes 196640 | tf_op jit(solution)/shard_map/ppermute | solution.py:31
  179.3 15.8 %collective-permute-done.11 = bf16[8,16,24,32]{3,0,2,1:T(8,128)(2,1)S(1)} collective-permute-done((bf16[8,16,24,32]{3,0,2,1:T(8,128)(2,1)S(1)}, bf16[8,16,24,32]{3,0,2,1:T(8,128)(2,1)S(1)}, u32[]{:S(2)}, u32[]{:S(2)}) %collective-permute-start.11) | collective-permute-done | bytes 196640 | tf_op jit(solution)/shard_map/ppermute | solution.py:31
  195.1 16.7 %collective-permute-done.12 = bf16[8,16,24,32]{3,0,2,1:T(8,128)(2,1)S(1)} collective-permute-done((bf16[8,16,24,32]{3,0,2,1:T(8,128)(2,1)S(1)}, bf16[8,16,24,32]{3,0,2,1:T(8,128)(2,1)S(1)}, u32[]{:S(2)}, u32[]{:S(2)}) %collective-permute-start.12) | collective-permute-done | bytes 196640 | tf_op jit(solution)/shard_map/ppermute | solution.py:31
  211.9 16.8 %collective-permute-done.13 = bf16[8,16,24,32]{3,0,2,1:T(8,128)(2,1)S(1)} collective-permute-done((bf16[8,16,24,32]{3,0,2,1:T(8,128)(2,1)S(1)}, bf16[8,16,24,32]{3,0,2,1:T(8,128)(2,1)S(1)}, u32[]{:S(2)}, u32[]{:S(2)}) %collective-permute-start.13) | collective-permute-done | bytes 196640 | tf_op jit(solution)/shard_map/ppermute | solution.py:31
  229.8 15.8 %collective-permute-done.14 = bf16[8,16,24,32]{3,0,2,1:T(8,128)(2,1)S(1)} collective-permute-done((bf16[8,16,24,32]{3,0,2,1:T(8,128)(2,1)S(1)}, bf16[8,16,24,32]{3,0,2,1:T(8,128)(2,1)S(1)}, u32[]{:S(2)}, u32[]{:S(2)}) %collective-permute-start.14) | collective-permute-done | bytes 196640 | tf_op jit(solution)/shard_map/ppermute | solution.py:31
  245.6 16.8 %collective-permute-done.15 = bf16[8,16,24,32]{3,0,2,1:T(8,128)(2,1)S(1)} collective-permute-done((bf16[8,16,24,32]{3,0,2,1:T(8,128)(2,1)S(1)}, bf16[8,16,24,32]{3,0,2,1:T(8,128)(2,1)S(1)}, u32[]{:S(2)}, u32[]{:S(2)}) %collective-permute-start.15) | collective-permute-done | bytes 196640 | tf_op jit(solution)/shard_map/ppermute | solution.py:31
  263.5 15.8 %collective-permute-done.16 = bf16[8,16,24,32]{3,0,2,1:T(8,128)(2,1)S(1)} collective-permute-done((bf16[8,16,24,32]{3,0,2,1:T(8,128)(2,1)S(1)}, bf16[8,16,24,32]{3,0,2,1:T(8,128)(2,1)S(1)}, u32[]{:S(2)}, u32[]{:S(2)}) %collective-permute-start.16) | collective-permute-done | bytes 196640 | tf_op jit(solution)/shard_map/ppermute | solution.py:31
  290.7 3.8 %collective-permute-done.17 = bf16[8,16,24,32]{3,0,2,1:T(8,128)(2,1)S(1)} collective-permute-done((bf16[8,16,24,32]{3,0,2,1:T(8,128)(2,1)S(1)}, bf16[8,16,24,32]{3,0,2,1:T(8,128)(2,1)S(1)}, u32[]{:S(2)}, u32[]{:S(2)}) %collective-permute-start.17) | collective-permute-done | bytes 196640 | tf_op jit(solution)/shard_map/ppermute | solution.py:31
  294.5 5.6 %fusion.12 = bf16[8,16,24,32]{3,0,2,1:T(8,128)(2,1)S(1)} fusion(f32[16,24,8,32]{3,2,1,0:T(8,128)S(1)} %fusion.49, f32[16,24,8,32]{3,2,1,0:T(8,128)S(1)} %fusion.51, f32[16,24,8,32]{3,2,1,0:T(8,128)S(1)} %fusion.53, f32[16,24,8,32]{3,2,1,0:T(8,128)S(1)} %fusion.55, f32[16,24,8,32]{3,2,1,0:T(8,128)S(1)} %fusion.57, f32[16,24,8,32]{3,2,1,0:T(8,128)S(1)} %fusion.59, ...), kind=kOutput, calls=%fused_computation.19 | convolution fusion | flops 3293184 | bytes 3366912 | tf_op jit(solution)/shard_map/ghmk,kghd->ghmd/dot_general | solution.py:54
  301.5 7.7 %all_to_all.27 = bf16[32,4,768]{2,1,0:T(4,128)(2,1)S(1)} all-to-all(bf16[32,4,768]{2,1,0:T(4,128)(2,1)S(1)} %reshape.305), channel_id=1, replica_groups=mesh['lon'=8,'lat'=4] {'lat'}, dimensions={0} | all-to-all | bytes 393216 | tf_op jit(solution)/shard_map/all_to_all | solution.py:133
  (133 shorter events, 51.1 us)
Async XLA Ops:
  0.0 300.7 %copy-start = (bf16[768,768]{1,0:T(8,128)(2,1)S(1)}, bf16[768,768]{1,0:T(8,128)(2,1)}, u32[]{:S(2)}) copy-start(bf16[768,768]{1,0:T(8,128)(2,1)} %param.18) | copy-start | bytes 3538948
  1.1 9.9 %collective-permute-start = (bf16[1,16,3072]{2,1,0:T(8,128)(2,1)S(1)}, bf16[1,16,3072]{2,1,0:T(8,128)(2,1)S(1)}, u32[]{:S(2)}, u32[]{:S(2)}) collective-permute-start(bf16[1,16,3072]{2,1,0:T(8,128)(2,1)S(1)} %get-tuple-element.24), channel_id=1, source_target_pairs={{0,1},{1,2},{2,3},{4,5},{5,6},{6,7},{8,9},{9,10},{10,11},{12,13},{... | collective-permute-start | bytes 294920 | tf_op jit(solution)/shard_map/ppermute | solution.py:20
  3.5 7.6 %collective-permute-start.1 = (bf16[1,16,3072]{2,1,0:T(8,128)(2,1)S(1)}, bf16[1,16,3072]{2,1,0:T(8,128)(2,1)S(1)}, u32[]{:S(2)}, u32[]{:S(2)}) collective-permute-start(bf16[1,16,3072]{2,1,0:T(8,128)(2,1)S(1)} %get-tuple-element.23), channel_id=1, source_target_pairs={{1,0},{2,1},{3,2},{5,4},{6,5},{7,6},{9,8},{10,9},{11,10},{13,12},{... | collective-permute-start | bytes 294920 | tf_op jit(solution)/shard_map/ppermute | solution.py:22
  11.3 15.9 %collective-permute-start.2 = (bf16[10,1,3072]{2,1,0:T(2,128)(2,1)S(1)}, bf16[10,1,3072]{2,1,0:T(2,128)(2,1)}, u32[]{:S(2)}, u32[]{:S(2)}) collective-permute-start(bf16[10,1,3072]{2,1,0:T(2,128)(2,1)S(1)} %get-tuple-element.21), channel_id=1, source_target_pairs={{0,4},{4,8},{8,12},{12,16},{16,20},{20,24},{24,28},{28,0},{1,5},{5... | collective-permute-start | bytes 184328 | tf_op jit(solution)/shard_map/ppermute | solution.py:20
  13.7 13.5 %collective-permute-start.3 = (bf16[10,1,3072]{2,1,0:T(2,128)(2,1)S(1)}, bf16[10,1,3072]{2,1,0:T(2,128)(2,1)}, u32[]{:S(2)}, u32[]{:S(2)}) collective-permute-start(bf16[10,1,3072]{2,1,0:T(2,128)(2,1)S(1)} %get-tuple-element.22), channel_id=1, source_target_pairs={{4,0},{8,4},{12,8},{16,12},{20,16},{24,20},{28,24},{0,28},{5,1},{9... | collective-permute-start | bytes 184328 | tf_op jit(solution)/shard_map/ppermute | solution.py:22
  34.2 10.7 %all-to-all-start = ((bf16[8,16,768]{2,0,1:T(8,128)(2,1)}), bf16[8,16,768]{2,0,1:T(8,128)(2,1)S(1)}, u32[]{:S(2)}, u32[]{:S(2)}) async-start(bf16[8,16,768]{2,0,1:T(8,128)(2,1)} %copy.136), calls=%async_computation | async-start | bytes 393216 | tf_op jit(solution)/shard_map/all_to_all | solution.py:82
  53.7 23.4 %collective-permute-start.4 = (bf16[8,16,24,32]{3,0,2,1:T(8,128)(2,1)}, bf16[8,16,24,32]{3,0,2,1:T(8,128)(2,1)}, u32[]{:S(2)}, u32[]{:S(2)}) collective-permute-start(bf16[8,16,24,32]{3,0,2,1:T(8,128)(2,1)} %copy.146), channel_id=1, source_target_pairs={{0,4},{4,8},{8,12},{12,16},{16,20},{20,24},{24,28},{28,0},{1,5},{5... | collective-permute-start | bytes 589832 | tf_op jit(solution)/shard_map/ppermute | solution.py:31
  55.8 38.1 %collective-permute-start.5 = (bf16[8,16,24,32]{3,0,2,1:T(8,128)(2,1)S(1)}, bf16[8,16,24,32]{3,0,2,1:T(8,128)(2,1)S(1)}, u32[]{:S(2)}, u32[]{:S(2)}) collective-permute-start(bf16[8,16,24,32]{3,0,2,1:T(8,128)(2,1)S(1)} %copy.150), channel_id=1, source_target_pairs={{0,4},{4,8},{8,12},{12,16},{16,20},{20,24},{24,28},{28,0},{1,5},{5... | collective-permute-start | bytes 589832 | tf_op jit(solution)/shard_map/ppermute | solution.py:31
  58.5 69.1 %copy-start.9 = (f32[24,8,8]{1,2,0:T(8,128)S(1)}, f32[24,8,8]{1,2,0:T(8,128)}, u32[]{:S(2)}) copy-start(f32[24,8,8]{1,2,0:T(8,128)} %copy.159) | copy-start | bytes 18436
  77.2 33.6 %collective-permute-start.6 = (bf16[8,16,24,32]{3,0,2,1:T(8,128)(2,1)}, bf16[8,16,24,32]{3,0,2,1:T(8,128)(2,1)S(1)}, u32[]{:S(2)}, u32[]{:S(2)}) collective-permute-start(bf16[8,16,24,32]{3,0,2,1:T(8,128)(2,1)} %collective-permute-done.4), channel_id=1, source_target_pairs={{0,4},{4,8},{8,12},{12,16},{16,20},{20,24},{24,28},{28,0},{1,5},{5... | collective-permute-start | bytes 589832 | tf_op jit(solution)/shard_map/ppermute | solution.py:31
  93.9 33.7 %collective-permute-start.7 = (bf16[8,16,24,32]{3,0,2,1:T(8,128)(2,1)S(1)}, bf16[8,16,24,32]{3,0,2,1:T(8,128)(2,1)S(1)}, u32[]{:S(2)}, u32[]{:S(2)}) collective-permute-start(bf16[8,16,24,32]{3,0,2,1:T(8,128)(2,1)S(1)} %collective-permute-done.5), channel_id=1, source_target_pairs={{0,4},{4,8},{8,12},{12,16},{16,20},{20,24},{24,28},{28,0},{1,5},{5... | collective-permute-start | bytes 589832 | tf_op jit(solution)/shard_map/ppermute | solution.py:31
  96.1 65.2 %copy-start.8 = (f32[24,8,8]{1,2,0:T(8,128)S(1)}, f32[24,8,8]{1,2,0:T(8,128)}, u32[]{:S(2)}) copy-start(f32[24,8,8]{1,2,0:T(8,128)} %copy.163) | copy-start | bytes 18436
  110.8 33.7 %collective-permute-start.8 = (bf16[8,16,24,32]{3,0,2,1:T(8,128)(2,1)S(1)}, bf16[8,16,24,32]{3,0,2,1:T(8,128)(2,1)S(1)}, u32[]{:S(2)}, u32[]{:S(2)}) collective-permute-start(bf16[8,16,24,32]{3,0,2,1:T(8,128)(2,1)S(1)} %collective-permute-done.6), channel_id=1, source_target_pairs={{0,4},{4,8},{8,12},{12,16},{16,20},{20,24},{24,28},{28,0},{1,5},{5... | collective-permute-start | bytes 589832 | tf_op jit(solution)/shard_map/ppermute | solution.py:31
  127.6 33.7 %collective-permute-start.9 = (bf16[8,16,24,32]{3,0,2,1:T(8,128)(2,1)S(1)}, bf16[8,16,24,32]{3,0,2,1:T(8,128)(2,1)S(1)}, u32[]{:S(2)}, u32[]{:S(2)}) collective-permute-start(bf16[8,16,24,32]{3,0,2,1:T(8,128)(2,1)S(1)} %collective-permute-done.7), channel_id=1, source_target_pairs={{0,4},{4,8},{8,12},{12,16},{16,20},{20,24},{24,28},{28,0},{1,5},{5... | collective-permute-start | bytes 589832 | tf_op jit(solution)/shard_map/ppermute | solution.py:31
  144.5 33.7 %collective-permute-start.10 = (bf16[8,16,24,32]{3,0,2,1:T(8,128)(2,1)S(1)}, bf16[8,16,24,32]{3,0,2,1:T(8,128)(2,1)S(1)}, u32[]{:S(2)}, u32[]{:S(2)}) collective-permute-start(bf16[8,16,24,32]{3,0,2,1:T(8,128)(2,1)S(1)} %collective-permute-done.8), channel_id=1, source_target_pairs={{0,4},{4,8},{8,12},{12,16},{16,20},{20,24},{24,28},{28,0},{1,5},{5... | collective-permute-start | bytes 589832 | tf_op jit(solution)/shard_map/ppermute | solution.py:31
  161.3 33.7 %collective-permute-start.11 = (bf16[8,16,24,32]{3,0,2,1:T(8,128)(2,1)S(1)}, bf16[8,16,24,32]{3,0,2,1:T(8,128)(2,1)S(1)}, u32[]{:S(2)}, u32[]{:S(2)}) collective-permute-start(bf16[8,16,24,32]{3,0,2,1:T(8,128)(2,1)S(1)} %collective-permute-done.9), channel_id=1, source_target_pairs={{0,4},{4,8},{8,12},{12,16},{16,20},{20,24},{24,28},{28,0},{1,5},{5... | collective-permute-start | bytes 589832 | tf_op jit(solution)/shard_map/ppermute | solution.py:31
  178.2 33.7 %collective-permute-start.12 = (bf16[8,16,24,32]{3,0,2,1:T(8,128)(2,1)S(1)}, bf16[8,16,24,32]{3,0,2,1:T(8,128)(2,1)S(1)}, u32[]{:S(2)}, u32[]{:S(2)}) collective-permute-start(bf16[8,16,24,32]{3,0,2,1:T(8,128)(2,1)S(1)} %collective-permute-done.10), channel_id=1, source_target_pairs={{0,4},{4,8},{8,12},{12,16},{16,20},{20,24},{24,28},{28,0},{1,5},{5... | collective-permute-start | bytes 589832 | tf_op jit(solution)/shard_map/ppermute | solution.py:31
  195.0 33.7 %collective-permute-start.13 = (bf16[8,16,24,32]{3,0,2,1:T(8,128)(2,1)S(1)}, bf16[8,16,24,32]{3,0,2,1:T(8,128)(2,1)S(1)}, u32[]{:S(2)}, u32[]{:S(2)}) collective-permute-start(bf16[8,16,24,32]{3,0,2,1:T(8,128)(2,1)S(1)} %collective-permute-done.11), channel_id=1, source_target_pairs={{0,4},{4,8},{8,12},{12,16},{16,20},{20,24},{24,28},{28,0},{1,5},{5... | collective-permute-start | bytes 589832 | tf_op jit(solution)/shard_map/ppermute | solution.py:31
  195.1 67.3 %copy-start.6 = (f32[24,8,8]{1,2,0:T(8,128)S(1)}, f32[24,8,8]{1,2,0:T(8,128)}, u32[]{:S(2)}) copy-start(f32[24,8,8]{1,2,0:T(8,128)} %copy.175) | copy-start | bytes 18436
  211.9 33.7 %collective-permute-start.14 = (bf16[8,16,24,32]{3,0,2,1:T(8,128)(2,1)S(1)}, bf16[8,16,24,32]{3,0,2,1:T(8,128)(2,1)S(1)}, u32[]{:S(2)}, u32[]{:S(2)}) collective-permute-start(bf16[8,16,24,32]{3,0,2,1:T(8,128)(2,1)S(1)} %collective-permute-done.12), channel_id=1, source_target_pairs={{0,4},{4,8},{8,12},{12,16},{16,20},{20,24},{24,28},{28,0},{1,5},{5... | collective-permute-start | bytes 589832 | tf_op jit(solution)/shard_map/ppermute | solution.py:31
  228.7 33.7 %collective-permute-start.15 = (bf16[8,16,24,32]{3,0,2,1:T(8,128)(2,1)S(1)}, bf16[8,16,24,32]{3,0,2,1:T(8,128)(2,1)S(1)}, u32[]{:S(2)}, u32[]{:S(2)}) collective-permute-start(bf16[8,16,24,32]{3,0,2,1:T(8,128)(2,1)S(1)} %collective-permute-done.13), channel_id=1, source_target_pairs={{0,4},{4,8},{8,12},{12,16},{16,20},{20,24},{24,28},{28,0},{1,5},{5... | collective-permute-start | bytes 589832 | tf_op jit(solution)/shard_map/ppermute | solution.py:31
  229.8 49.5 %copy-start.4 = (f32[24,8,8]{1,2,0:T(8,128)S(1)}, f32[24,8,8]{1,2,0:T(8,128)}, u32[]{:S(2)}) copy-start(f32[24,8,8]{1,2,0:T(8,128)} %copy.179) | copy-start | bytes 18436
  245.6 33.7 %collective-permute-start.16 = (bf16[8,16,24,32]{3,0,2,1:T(8,128)(2,1)S(1)}, bf16[8,16,24,32]{3,0,2,1:T(8,128)(2,1)S(1)}, u32[]{:S(2)}, u32[]{:S(2)}) collective-permute-start(bf16[8,16,24,32]{3,0,2,1:T(8,128)(2,1)S(1)} %collective-permute-done.14), channel_id=1, source_target_pairs={{0,4},{4,8},{8,12},{12,16},{16,20},{20,24},{24,28},{28,0},{1,5},{5... | collective-permute-start | bytes 589832 | tf_op jit(solution)/shard_map/ppermute | solution.py:31
  262.4 32.0 %collective-permute-start.17 = (bf16[8,16,24,32]{3,0,2,1:T(8,128)(2,1)S(1)}, bf16[8,16,24,32]{3,0,2,1:T(8,128)(2,1)S(1)}, u32[]{:S(2)}, u32[]{:S(2)}) collective-permute-start(bf16[8,16,24,32]{3,0,2,1:T(8,128)(2,1)S(1)} %collective-permute-done.15), channel_id=1, source_target_pairs={{0,4},{4,8},{8,12},{12,16},{16,20},{20,24},{24,28},{28,0},{1,5},{5... | collective-permute-start | bytes 589832 | tf_op jit(solution)/shard_map/ppermute | solution.py:31
  (13 other events, 210.4 us)
where the time goes:
time: 311 us; the launch traced here: 310 us
  waiting for transfers between devices  221 us (71%)
  matrix products  33.6 us (11%)
  local copies, waits for them, and re-layouts  23.8 us (8%)
  starting transfers between devices  15.9 us (5%)
  blocking collectives  7.67 us (2%)
  other arithmetic  7.35 us (2%)
    ppermute x14, waiting for transfers between devices, shifted(): return lax.ppermute(x, axis, [(i, (i + by) % peers) for i in range(peers)])  217 us
    dot_general x8, matrix products, absorb(): jnp.einsum('ghmk,kghd->ghmd', weights.astype(jnp.bfloat16), values, prefe...  10.4 us
    dot_general x8, matrix products, absorb(): jnp.einsum('mghd,kghd->ghmk', queries, keys, preferred_element_type=jnp.f...  10.1 us
    all_to_all x1, blocking collectives, local(): lax.all_to_all(result, 'lat', split_axis=0, concat_axis=1, tiled=True)  7.67 us
    dot_general x8, local copies, waits for them, and re-layouts, spread_bias(): return jnp.einsum('hs,mks->hmk', table_hop, choose)  7.43 us
    dot_general x1, matrix products, local(): jnp.dot(activated.reshape(-1, width_exp), w_proj, preferred_element_type=...  6.27 us
  transfers between devices with their start and end apart: 19, of which 15 were waited for; matrix products, arithmetic and copies ran while one was open for 13% of the time, Pallas kernels for 0%

commit v1 on v0

v1 whole, which is shorter than its diff:
```python
import jax
import jax.numpy as jnp
from jax import lax
from jax.sharding import PartitionSpec as P

GRID = 8


eps = 1e-05


def padded(cells, sides, width, closed):
    for axis, dim in sides:
        count = lax.axis_size(axis)
        ends = count if closed else count - 1
        head = lax.slice_in_dim(cells, 0, width, axis=dim)
        tail = lax.slice_in_dim(cells, cells.shape[dim] - width, cells.shape[dim], axis=dim)
        cells = jnp.concatenate(
            [
                lax.ppermute(tail, axis, [(i, (i + 1) % count) for i in range(ends)]),
                cells,
                lax.ppermute(head, axis, [((i + 1) % count, i) for i in range(ends)]),
            ],
            axis=dim,
        )
    return cells


def exchange(x, stride):
    if stride == 1:
        return lax.all_to_all(x, ("lat", "lon"), split_axis=0, concat_axis=0, tiled=True)
    lats = lax.axis_size("lat")
    lons = lax.axis_size("lon")
    teams = [[s + stride * n for n in range(lons // stride)] for s in range(stride)]
    x = x.reshape((lats, lons // stride) + x.shape[1:])
    x = lax.all_to_all(x, "lat", split_axis=0, concat_axis=0, tiled=True)
    x = lax.all_to_all(x, "lon", split_axis=1, concat_axis=1, tiled=True, axis_index_groups=teams)
    return x.reshape((-1,) + x.shape[2:])


def full_bias(rel_bias):
    heads = rel_bias.shape[0]
    turned = jnp.stack([jnp.roll(rel_bias, n, axis=2) for n in range(GRID)], axis=1)
    rows = [turned[:, :, GRID - 1 - m : 2 * GRID - 1 - m] for m in range(GRID)]
    return jnp.stack(rows, axis=1).reshape(heads, GRID * GRID, GRID * GRID)


def local(expanded, stream, land, polar, land_shift, dw_kernel, w_proj, w_qkv, w_out, rel_bias):
    rows_dev, cols_dev, width_exp = expanded.shape
    width = stream.shape[2]
    heads = rel_bias.shape[0]
    head_dim = width // heads
    extended = padded(expanded, (("lat", 0),), 1, False)
    extended = padded(extended, (("lon", 1),), 1, True)
    filtered = land[:, :, None].astype(jnp.float32) * land_shift[None, None, :]
    for row_tap in range(3):
        for col_tap in range(3):
            filtered = (
                filtered
                + extended[row_tap : row_tap + rows_dev, col_tap : col_tap + cols_dev]
                * dw_kernel[row_tap, col_tap]
            )
    activated = jax.nn.gelu(filtered).astype(jnp.bfloat16)
    projected = jnp.dot(
        activated.reshape(-1, width_exp), w_proj, preferred_element_type=jnp.float32
    )
    mixed = (stream.astype(jnp.float32) + projected.reshape(rows_dev, cols_dev, width)).astype(
        jnp.bfloat16
    )
    flat = mixed.reshape(-1, width).astype(jnp.float32)
    centre = jnp.mean(flat, axis=1, keepdims=True)
    centred = flat - centre
    spread = jnp.mean(centred * centred, axis=1, keepdims=True)
    normed = (centred * lax.rsqrt(spread + eps)).astype(jnp.bfloat16)
    lats = lax.axis_size("lat")
    stride = lax.axis_size("lon") // GRID
    halves = GRID // lats
    strip = rows_dev // halves
    assert strip == lats
    packs = cols_dev // GRID
    sent = normed.reshape(halves, strip, packs, GRID, width)
    sent = jnp.transpose(sent, (1, 3, 0, 2, 4)).reshape(lats * GRID, halves * packs, width)
    here = exchange(sent, stride).reshape(lats, GRID, halves, packs, width)
    tokens = jnp.transpose(here, (3, 0, 2, 1, 4)).reshape(-1, width)
    qkv = jnp.dot(tokens, w_qkv, preferred_element_type=jnp.float32).astype(jnp.bfloat16)
    qkv = qkv.reshape(packs, GRID * GRID, 3, heads, head_dim)
    scores = jnp.einsum(
        "gqhd,gkhd->ghqk", qkv[:, :, 0], qkv[:, :, 1], preferred_element_type=jnp.float32
    ) * head_dim ** (-0.5) + full_bias(rel_bias)
    caps = lax.dynamic_index_in_dim(
        polar.reshape(GRID, strip), lax.axis_index("lat"), 1, keepdims=False
    )
    scores = jnp.where(jnp.repeat(caps == 0, GRID), scores, -1e30)
    weights = jnp.exp(scores - jnp.max(scores, axis=-1, keepdims=True))
    probs = (weights / jnp.sum(weights, axis=-1, keepdims=True)).astype(jnp.bfloat16)
    attended = jnp.einsum(
        "ghqk,gkhd->gqhd", probs, qkv[:, :, 2], preferred_element_type=jnp.float32
    ).astype(jnp.bfloat16)
    back = attended.reshape(packs, lats, halves, GRID, width)
    back = jnp.transpose(back, (1, 3, 2, 0, 4)).reshape(lats * GRID, halves * packs, width)
    home = exchange(back, stride).reshape(strip, GRID, halves, packs, width)
    home = jnp.transpose(home, (2, 0, 3, 1, 4)).reshape(-1, width)
    result = flat + jnp.dot(home, w_out, preferred_element_type=jnp.float32)
    return result.astype(jnp.bfloat16).reshape(rows_dev, cols_dev, width)


def solution(mesh):
    in_specs = (
        P("lat", "lon", None),
        P("lat", "lon", None),
        P("lat", "lon"),
        P(),
        P(),
        P(),
        P(),
        P(),
        P(),
        P(),
    )
    out_specs = P("lat", "lon", None)
    return jax.shard_map(local, mesh=mesh, in_specs=in_specs, out_specs=out_specs, check_vma=False)
```

time: 311 us -> 89.3 us (0.29)
  waiting for transfers between devices: 221 us -> 3.82 us
  matrix products: 33.6 us -> 14.6 us
  local copies, waits for them, and re-layouts: 23.8 us -> 37.1 us
  blocking collectives: 7.67 us -> 13.1 us
  other arithmetic: 7.35 us -> 2.62 us
    ppermute x14 -> x0, waiting for transfers between devices: 217 us -> none  [shifted(): return lax.ppermute(x, axis, [(i, (i + by) % peers) for i in range(peers)])]
    dot_general x27 -> x4, matrix products: 27.4 us -> 7.4 us  [the longest x1 3.28 us: local(): jnp.einsum('ghqk,gkhd->gqhd', probs, qkv[:, :, 2], preferred_element_type...]
    dot_general x8 -> x0, local copies, waits for them, and re-layouts: 7.43 us -> none  [spread_bias(): return jnp.einsum('hs,mks->hmk', table_hop, choose)]
    slice x2 -> x8, local copies, waits for them, and re-layouts: 2.57 us -> 9.46 us  [the longest x7 6.42 us: full_bias(): jnp.roll(rel_bias, n, axis=2)]
    all_to_all x1, blocking collectives: 7.67 us -> 13.1 us  [exchange(): lax.all_to_all(x, ('lat', 'lon'), split_axis=0, concat_axis=0, tiled=True)]
    unnamed x38 -> x40, local copies, waits for them, and re-layouts: 0.52 us -> 5.94 us
    reduce_sum x5 -> x0, other arithmetic: 5.27 us -> none  [the longest x4 5.02 us: absorb(): total = total * factor + jnp.sum(weights, axis=-1)]
    all_to_all x1, waiting for transfers between devices: 4.36 us -> 0.54 us  [exchange(): lax.all_to_all(x, ('lat', 'lon'), split_axis=0, concat_axis=0, tiled=True)]
  transfers between devices with their start and end apart: 19 -> 5, of which waited for: 15 -> 3; matrix products, arithmetic and copies ran while one was open for 13% -> 17% of each run, Pallas kernels for 0% -> 0%
where the time goes in v1:
time: 89.3 us; the launch traced here: 88.2 us
  local copies, waits for them, and re-layouts  37.1 us (42%)
  starting transfers between devices  16.5 us (18%)
  matrix products  14.6 us (16%)
  blocking collectives  13.1 us (15%)
  waiting for transfers between devices  3.82 us (4%)
  other arithmetic  2.62 us (3%)
    all_to_all x1, blocking collectives, exchange(): lax.all_to_all(x, ('lat', 'lon'), split_axis=0, concat_axis=0, tiled=True)  13.1 us
    all_to_all x1, starting transfers between devices, exchange(): lax.all_to_all(x, ('lat', 'lon'), split_axis=0, concat_axis=0, tiled=True)  7.24 us
    slice x7, local copies, waits for them, and re-layouts, full_bias(): jnp.roll(rel_bias, n, axis=2)  6.42 us
    unnamed x40, local copies, waits for them, and re-layouts  5.94 us
    ppermute x2, starting transfers between devices, padded(): lax.ppermute(tail, axis, [(i, (i + 1) % count) for i in range(ends)])  4.9 us
    dot_general x1, matrix products, local(): jnp.dot(activated.reshape(-1, width_exp), w_proj, preferred_element_type=...  4.41 us
    ppermute x2, starting transfers between devices, padded(): lax.ppermute(head, axis, [((i + 1) % count, i) for i in range(ends)])  4.4 us
    add x1, local copies, waits for them, and re-layouts, local(): jnp.einsum('gqhd,gkhd->ghqk', qkv[:, :, 0], qkv[:, :, 1], preferred_eleme...  3.73 us
  transfers between devices with their start and end apart: 5, of which 3 were waited for; matrix products, arithmetic and copies ran while one was open for 17% of the time, Pallas kernels for 0%

profile of v1, /device:TPU:0, one launch (start us, length us, event | category | flops | bytes accessed | tf_op | source)
XLA Modules:
  0.0 88.2 jit_solution(40407812105508165)
XLA Ops:
  1.1 2.5 %collective-permute-start = (bf16[1,16,3072]{2,1,0:T(8,128)(2,1)S(1)}, bf16[1,16,3072]{2,1,0:T(8,128)(2,1)S(1)}, u32[]{:S(2)}, u32[]{:S(2)}) collective-permute-start(bf16[1,16,3072]{2,1,0:T(8,128)(2,1)S(1)} %get-tuple-element.11), channel_id=1, source_target_pairs={{0,1},{1,2},{2,3},{4,5},{5,6},{6,7},{8,9},{9,10},{10,11},{12,13},{... | collective-permute-start | bytes 294920 | tf_op jit(solution)/shard_map/ppermute | solution.py:20
  3.7 1.3 %collective-permute-start.1 = (bf16[1,16,3072]{2,1,0:T(8,128)(2,1)S(1)}, bf16[1,16,3072]{2,1,0:T(8,128)(2,1)S(1)}, u32[]{:S(2)}, u32[]{:S(2)}) collective-permute-start(bf16[1,16,3072]{2,1,0:T(8,128)(2,1)S(1)} %get-tuple-element.10), channel_id=1, source_target_pairs={{1,0},{2,1},{3,2},{5,4},{6,5},{7,6},{9,8},{10,9},{11,10},{13,12},{... | collective-permute-start | bytes 294920 | tf_op jit(solution)/shard_map/ppermute | solution.py:22
  14.0 2.4 %collective-permute-start.2 = (bf16[10,1,3072]{2,1,0:T(2,128)(2,1)S(1)}, bf16[10,1,3072]{2,1,0:T(2,128)(2,1)S(1)}, u32[]{:S(2)}, u32[]{:S(2)}) collective-permute-start(bf16[10,1,3072]{2,1,0:T(2,128)(2,1)S(1)} %get-tuple-element.8), channel_id=1, source_target_pairs={{0,4},{4,8},{8,12},{12,16},{16,20},{20,24},{24,28},{28,0},{1,5},{5... | collective-permute-start | bytes 184328 | tf_op jit(solution)/shard_map/ppermute | solution.py:20
  16.4 3.1 %collective-permute-start.3 = (bf16[10,1,3072]{2,1,0:T(2,128)(2,1)S(1)}, bf16[10,1,3072]{2,1,0:T(2,128)(2,1)S(1)}, u32[]{:S(2)}, u32[]{:S(2)}) collective-permute-start(bf16[10,1,3072]{2,1,0:T(2,128)(2,1)S(1)} %get-tuple-element.9), channel_id=1, source_target_pairs={{4,0},{8,4},{12,8},{16,12},{20,16},{24,20},{28,24},{0,28},{5,1},{9... | collective-permute-start | bytes 184328 | tf_op jit(solution)/shard_map/ppermute | solution.py:22
  19.5 1.3 %copy-done.4 = f32[24,8,8,8,8]{0,4,3,2,1:T(8,128)} copy-done((f32[24,8,8,8,8]{0,4,3,2,1:T(8,128)}, f32[24,8,8,8,8]{0,4,3,2,1:T(8,128)S(1)}, u32[]{:S(2)}) %copy-start.4) | copy-done | bytes 393240
  20.8 1.6 %collective-permute-done.2 = bf16[10,1,3072]{2,1,0:T(2,128)(2,1)S(1)} collective-permute-done((bf16[10,1,3072]{2,1,0:T(2,128)(2,1)S(1)}, bf16[10,1,3072]{2,1,0:T(2,128)(2,1)S(1)}, u32[]{:S(2)}, u32[]{:S(2)}) %collective-permute-start.2) | collective-permute-done | bytes 61472 | tf_op jit(solution)/shard_map/ppermute | solution.py:20
  22.4 1.7 %collective-permute-done.3 = bf16[10,1,3072]{2,1,0:T(2,128)(2,1)S(1)} collective-permute-done((bf16[10,1,3072]{2,1,0:T(2,128)(2,1)S(1)}, bf16[10,1,3072]{2,1,0:T(2,128)(2,1)S(1)}, u32[]{:S(2)}, u32[]{:S(2)}) %collective-permute-start.3) | collective-permute-done | bytes 61472 | tf_op jit(solution)/shard_map/ppermute | solution.py:22
  24.1 4.4 %fusion.64 = (f32[8,16]{1,0:T(8,128)S(1)}, f32[8,16,768]{2,1,0:T(8,128)}) fusion(bf16[3072,768]{1,0:T(8,128)(2,1)S(1)} %copy-done.12, bf16[8,16,3072]{2,1,0:T(8,128)(2,1)S(1)} %copy-done.7, bf16[10,16,3072]{2,1,0:T(8,128)(2,1)S(1)} %constant_dynamic-update-slice_fusion, bf16[10,1,3072]{2,1,0:T(2,128)(2,1)S(1)} %collective-permute-done.3, ...), kind=kOutput, calls=%fused_computation.102 | convolution fusion | flops 628457344 | bytes 7521280 | tf_op jit(solution)/shard_map/dot_general | solution.py:64
  28.6 1.2 %multiply_reduce_fusion = f32[8,16]{1,0:T(8,128)S(1)} fusion(f32[8,16,768]{2,1,0:T(8,128)} %get-tuple-element.36, f32[8,16]{1,0:T(8,128)S(1)} %broadcast_multiply_fusion), kind=kLoop, calls=%fused_computation.46 | loop fusion | flops 294784 | bytes 394240 | tf_op jit(solution)/shard_map/reduce_sum | solution.py:73
  31.2 1.1 %fusion.30 = bf16[2,4,2,8,768]{4,3,1,2,0:T(8,128)(2,1)S(1)} fusion(f32[2,4,2,8,768]{4,3,2,1,0:T(8,128)} %bitcast.127, f32[2,4,2,8]{3,1,2,0:T(4,128)S(1)} %copy.44, f32[2,4,2,8]{3,1,2,0:T(4,128)S(1)} %copy.42), kind=kLoop, calls=%fused_computation.45 | loop fusion | flops 294912 | bytes 590848 | tf_op jit(solution)/shard_map/convert_element_type | solution.py:74
  33.1 7.2 %all-to-all-start = ((bf16[32,4,768]{2,1,0:T(4,128)(2,1)}), bf16[32,4,768]{2,1,0:T(4,128)(2,1)}, u32[]{:S(2)}, u32[]{:S(2)}) async-start(bf16[32,4,768]{2,1,0:T(4,128)(2,1)} %copy.45), calls=%async_computation | async-start | bytes 393216 | tf_op jit(solution)/shard_map/all_to_all | solution.py:31
  40.4 1.7 %fusion.32 = f32[24,8,8,8,8]{0,4,3,2,1:T(8,128)} fusion(f32[24,8,8,8,8]{0,4,3,2,1:T(8,128)} %copy-done.4, f32[24,8,15,8]{0,3,2,1:T(8,128)} %copy-done.1), kind=kLoop, calls=%fused_computation.50 | loop fusion | bytes 524288
  42.1 1.7 %fusion.31 = f32[24,8,8,8,8]{0,4,3,2,1:T(8,128)} fusion(f32[24,8,8,8,8]{0,4,3,2,1:T(8,128)} %fusion.32, f32[24,8,15,8]{0,3,2,1:T(8,128)} %copy-done.1), kind=kLoop, calls=%fused_computation.48 | loop fusion | bytes 524288 | tf_op jit(solution)/shard_map/stack | solution.py:45
  43.7 3.7 %copy.52 = f32[24,64,64]{1,2,0:T(8,128)} copy(f32[24,64,64]{0,2,1:T(8,128)} %bitcast.129) | data formatting | bytes 786432 | tf_op jit(solution)/shard_map/add | solution.py:87
  49.4 1.5 %convolution_convert_fusion = bf16[128,2304]{1,0:T(8,128)(2,1)} fusion(bf16[128,768]{1,0:T(8,128)(2,1)S(1)} %bitcast.130, bf16[768,2304]{1,0:T(8,128)(2,1)S(1)} %copy-done), kind=kOutput, calls=%fused_computation.3 | convolution fusion | flops 453279744 | bytes 4325376 | tf_op jit(solution)/shard_map/dot_general | solution.py:85
  50.9 2.1 %copy.48 = bf16[128,2304]{0,1:T(8,128)(2,1)} copy(bf16[128,2304]{1,0:T(8,128)(2,1)} %convolution_convert_fusion) | data formatting | bytes 1179648 | tf_op jit(solution)/shard_map/convert_element_type | solution.py:85
  53.1 3.4 %reshape.97 = bf16[2,64,3,24,32]{1,0,4,3,2:T(2,128)(2,1)} reshape(bf16[128,2304]{0,1:T(8,128)(2,1)} %copy.48) | data formatting | bytes 1179648 | tf_op jit(solution)/shard_map/reshape | solution.py:86
  56.4 3.0 %fusion.53 = (bf16[2,64,1,24,32]{1,0,4,3,2:T(2,128)(2,1)}, bf16[2,64,1,24,32]{1,0,4,3,2:T(2,128)(2,1)S(1)}, bf16[2,64,1,24,32]{1,0,4,3,2:T(2,128)(2,1)S(1)}) fusion(bf16[2,64,3,24,32]{1,0,4,3,2:T(2,128)(2,1)} %reshape.97), kind=kLoop, calls=%fused_computation.91 | loop fusion | bytes 1179648 | tf_op jit(solution)/shard_map/slice | solution.py:97
  60.4 1.6 %add_select_fusion = f32[2,24,64,64]{2,3,1,0:T(8,128)} fusion(f32[24,64,64]{1,2,0:T(8,128)S(1)} %copy-done.3, pred[64]{0:T(512)(128)(4,1)S(1)} %reshape.99, bf16[2,64,1,24,32]{1,0,4,3,2:T(2,128)(2,1)S(1)} %get-tuple-element.7, bf16[2,64,1,24,32]{1,0,4,3,2:T(2,128)(2,1)S(1)} %get-tuple-element.6), kind=kOutput, calls=%fused_computation.19 | convolution fusion | flops 13172736 | bytes 1572928 | tf_op jit(solution)/shard_map/gqhd,gkhd->ghqk/dot_general | solution.py:87
  62.0 2.8 %fusion.65 = f32[2,24,64]{2,1,0:T(8,128)} fusion(f32[24,64,64]{1,2,0:T(8,128)} %copy.52, pred[64]{0:T(512)(128)(4,1)S(1)} %reshape.99, bf16[2,64,1,24,32]{1,0,4,3,2:T(2,128)(2,1)} %copy-done.6, bf16[2,64,1,24,32]{1,0,4,3,2:T(2,128)(2,1)} %copy-done.5), kind=kOutput, calls=%fused_computation.103 | convolution fusion | flops 13566015 | bytes 798784 | tf_op jit(solution)/shard_map/sub | solution.py:94
  64.8 3.3 %fusion.13 = bf16[2,64,24,32]{1,3,2,0:T(8,128)(2,1)} fusion(f32[2,24,64]{2,1,0:T(8,128)} %fusion.65, bf16[2,64,1,24,32]{1,0,4,3,2:T(2,128)(2,1)} %get-tuple-element.5, f32[2,24,64,64]{2,3,1,0:T(8,128)} %add_select_fusion), kind=kOutput, calls=%fused_computation.26 | convolution fusion | flops 13274175 | bytes 1191936 | tf_op jit(solution)/shard_map/ghqk,gkhd->gqhd/dot_general | solution.py:96
  68.1 2.3 %copy.54 = bf16[2,64,24,32]{3,2,1,0:T(8,128)(2,1)} copy(bf16[2,64,24,32]{1,3,2,0:T(8,128)(2,1)} %fusion.13) | data formatting | bytes 393216 | tf_op jit(solution)/shard_map/convert_element_type | solution.py:98
  70.4 2.3 %reshape.100 = bf16[2,4,2,8,768]{4,3,2,1,0:T(8,128)(2,1)} reshape(bf16[2,64,24,32]{3,2,1,0:T(8,128)(2,1)} %copy.54) | data formatting | bytes 393216 | tf_op jit(solution)/shard_map/reshape | solution.py:99
  74.0 13.1 %all_to_all.10 = bf16[32,4,768]{2,1,0:T(4,128)(2,1)S(1)} all-to-all(bf16[32,4,768]{2,1,0:T(4,128)(2,1)S(1)} %copy.56), channel_id=1, replica_groups=mesh['lon'=8,'lat'=4] {'lat','lon'}, dimensions={0} | all-to-all | bytes 393216 | tf_op jit(solution)/shard_map/all_to_all | solution.py:31
  (78 shorter events, 17.4 us)
Async XLA Ops:
  0.0 49.4 %copy-start = (bf16[768,2304]{1,0:T(8,128)(2,1)S(1)}, bf16[768,2304]{1,0:T(8,128)(2,1)}, u32[]{:S(2)}) copy-start(bf16[768,2304]{1,0:T(8,128)(2,1)} %param.17) | copy-start | bytes 10616836
  1.1 12.2 %collective-permute-start = (bf16[1,16,3072]{2,1,0:T(8,128)(2,1)S(1)}, bf16[1,16,3072]{2,1,0:T(8,128)(2,1)S(1)}, u32[]{:S(2)}, u32[]{:S(2)}) collective-permute-start(bf16[1,16,3072]{2,1,0:T(8,128)(2,1)S(1)} %get-tuple-element.11), channel_id=1, source_target_pairs={{0,1},{1,2},{2,3},{4,5},{5,6},{6,7},{8,9},{9,10},{10,11},{12,13},{... | collective-permute-start | bytes 294920 | tf_op jit(solution)/shard_map/ppermute | solution.py:20
  3.7 10.2 %collective-permute-start.1 = (bf16[1,16,3072]{2,1,0:T(8,128)(2,1)S(1)}, bf16[1,16,3072]{2,1,0:T(8,128)(2,1)S(1)}, u32[]{:S(2)}, u32[]{:S(2)}) collective-permute-start(bf16[1,16,3072]{2,1,0:T(8,128)(2,1)S(1)} %get-tuple-element.10), channel_id=1, source_target_pairs={{1,0},{2,1},{3,2},{5,4},{6,5},{7,6},{9,8},{10,9},{11,10},{13,12},{... | collective-permute-start | bytes 294920 | tf_op jit(solution)/shard_map/ppermute | solution.py:22
  12.2 0.9 %copy-start.9 = (f32[3,3,3072]{2,1,0:T(4,128)S(1)}, f32[3,3,3072]{2,1,0:T(4,128)}, u32[]{:S(2)}) copy-start(f32[3,3,3072]{2,1,0:T(4,128)} %param.15) | copy-start | bytes 331780
  12.4 1.3 %copy-start.7 = (bf16[8,16,3072]{2,1,0:T(8,128)(2,1)S(1)}, bf16[8,16,3072]{2,1,0:T(8,128)(2,1)}, u32[]{:S(2)}) copy-start(bf16[8,16,3072]{2,1,0:T(8,128)(2,1)} %param.10) | copy-start | bytes 2359300
  12.5 7.0 %copy-start.1 = (f32[24,8,15,8]{0,3,2,1:T(8,128)}, f32[24,8,15,8]{0,3,2,1:T(8,128)S(1)}, u32[]{:S(2)}) copy-start(f32[24,8,15,8]{0,3,2,1:T(8,128)S(1)} %fusion.45) | copy-start | bytes 276484
  12.5 11.6 %copy-start.13 = (bf16[8,16,768]{2,1,0:T(8,128)(2,1)S(1)}, bf16[8,16,768]{2,1,0:T(8,128)(2,1)}, u32[]{:S(2)}) copy-start(bf16[8,16,768]{2,1,0:T(8,128)(2,1)} %param.11) | copy-start | bytes 589828
  12.5 11.6 %copy-start.12 = (bf16[3072,768]{1,0:T(8,128)(2,1)S(1)}, bf16[3072,768]{1,0:T(8,128)(2,1)}, u32[]{:S(2)}) copy-start(bf16[3072,768]{1,0:T(8,128)(2,1)} %param.16) | copy-start | bytes 14155780
  13.3 7.6 %copy-start.10 = (s32[8,16]{1,0:T(8,128)S(1)}, s32[8,16]{1,0:T(8,128)}, u32[]{:S(2)}) copy-start(s32[8,16]{1,0:T(8,128)} %param.12) | copy-start | bytes 1540
  13.3 10.8 %copy-start.14 = (f32[3072]{0:T(1024)S(1)}, f32[3072]{0:T(1024)}, u32[]{:S(2)}) copy-start(f32[3072]{0:T(1024)} %param.14) | copy-start | bytes 36868
  14.0 8.4 %collective-permute-start.2 = (bf16[10,1,3072]{2,1,0:T(2,128)(2,1)S(1)}, bf16[10,1,3072]{2,1,0:T(2,128)(2,1)S(1)}, u32[]{:S(2)}, u32[]{:S(2)}) collective-permute-start(bf16[10,1,3072]{2,1,0:T(2,128)(2,1)S(1)} %get-tuple-element.8), channel_id=1, source_target_pairs={{0,4},{4,8},{8,12},{12,16},{16,20},{20,24},{24,28},{28,0},{1,5},{5... | collective-permute-start | bytes 184328 | tf_op jit(solution)/shard_map/ppermute | solution.py:20
  16.4 7.7 %collective-permute-start.3 = (bf16[10,1,3072]{2,1,0:T(2,128)(2,1)S(1)}, bf16[10,1,3072]{2,1,0:T(2,128)(2,1)S(1)}, u32[]{:S(2)}, u32[]{:S(2)}) collective-permute-start(bf16[10,1,3072]{2,1,0:T(2,128)(2,1)S(1)} %get-tuple-element.9), channel_id=1, source_target_pairs={{4,0},{8,4},{12,8},{16,12},{20,16},{24,20},{28,24},{0,28},{5,1},{9... | collective-permute-start | bytes 184328 | tf_op jit(solution)/shard_map/ppermute | solution.py:22
  19.5 1.3 %copy-start.4 = (f32[24,8,8,8,8]{0,4,3,2,1:T(8,128)}, f32[24,8,8,8,8]{0,4,3,2,1:T(8,128)S(1)}, u32[]{:S(2)}) copy-start(f32[24,8,8,8,8]{0,4,3,2,1:T(8,128)S(1)} %fusion.33) | copy-start | bytes 1179652
  33.1 15.3 %all-to-all-start = ((bf16[32,4,768]{2,1,0:T(4,128)(2,1)}), bf16[32,4,768]{2,1,0:T(4,128)(2,1)}, u32[]{:S(2)}, u32[]{:S(2)}) async-start(bf16[32,4,768]{2,1,0:T(4,128)(2,1)} %copy.45), calls=%async_computation | async-start | bytes 393216 | tf_op jit(solution)/shard_map/all_to_all | solution.py:31
  43.7 3.7 %copy-start.11 = (s32[32]{0:T(128)S(1)}, s32[32]{0:T(128)}, u32[]{:S(2)}) copy-start(s32[32]{0:T(128)} %param.13) | copy-start | bytes 388
  56.4 3.9 %copy-start.3 = (f32[24,64,64]{1,2,0:T(8,128)S(1)}, f32[24,64,64]{1,2,0:T(8,128)}, u32[]{:S(2)}) copy-start(f32[24,64,64]{1,2,0:T(8,128)} %copy.52) | copy-start | bytes 1179652
  59.5 0.8 copy-start.5
  59.5 0.9 %copy-start.6 = (bf16[2,64,1,24,32]{1,0,4,3,2:T(2,128)(2,1)}, bf16[2,64,1,24,32]{1,0,4,3,2:T(2,128)(2,1)S(1)}, u32[]{:S(2)}) copy-start(bf16[2,64,1,24,32]{1,0,4,3,2:T(2,128)(2,1)S(1)} %get-tuple-element.7) | copy-start | bytes 589828
  72.7 14.4 %copy-start.2 = (f32[8,16,768]{2,1,0:T(8,128)S(1)}, f32[8,16,768]{2,1,0:T(8,128)}, u32[]{:S(2)}) copy-start(f32[8,16,768]{2,1,0:T(8,128)} %get-tuple-element.36) | copy-start | bytes 1179652
  72.8 14.4 %copy-start.8 = (bf16[768,768]{1,0:T(8,128)(2,1)S(1)}, bf16[768,768]{1,0:T(8,128)(2,1)}, u32[]{:S(2)}) copy-start(bf16[768,768]{1,0:T(8,128)(2,1)} %param.18) | copy-start | bytes 3538948

commit v2 on v1

v2 whole, which is shorter than its diff:
```python
import functools

import jax
import jax.numpy as jnp
import numpy as np
from jax import lax
from jax.experimental import pallas as pl
from jax.experimental.pallas import tpu as pltpu
from jax.sharding import PartitionSpec as P

GRID = 8
LANES = 128
NEVER = -1e30

eps = 1e-05


def orders(rows, cols, lats):
    halves = GRID // lats
    packs = cols // GRID
    per = halves * packs
    count = rows * cols
    home = np.zeros((2 * count, 2 * count), np.float32)
    away = np.zeros((2 * count, 2 * count), np.float32)
    for lat in range(lats):
        for n in range(GRID):
            for a in range(halves):
                for g in range(packs):
                    for part in range(2):
                        slot = (lat * GRID + n) * 2 * per + part * per + a * packs + g
                        own = (a * lats + lat) * cols + g * GRID + n
                        group = (g * GRID + lat * halves + a) * GRID + n
                        home[slot, part * count + own] = 1
                        away[slot, part * count + group] = 1
    return home, away


def edge_picks(rows, cols):
    picks = np.zeros((6 * 8, rows * cols), np.float32)
    for r in range(rows):
        picks[r, r * cols] = 1
        picks[8 + r, r * cols + cols - 1] = 1
    picks[16, 0] = 1
    picks[24, cols - 1] = 1
    picks[32, (rows - 1) * cols] = 1
    picks[40, rows * cols - 1] = 1
    return picks


def kernel(
    lats,
    lons,
    heads,
    expanded,
    stream,
    w_proj,
    w_qkv,
    w_out,
    polar,
    land,
    shift,
    taps,
    table,
    picks,
    home,
    home_t,
    away,
    away_t,
    out,
    ext,
    edges,
    corners,
    side,
    corner_in,
    stream_v,
    wp,
    wq,
    wo,
    act,
    mixed,
    turned,
    bias,
    qkv,
    attended,
    sent1,
    came1,
    sent2,
    came2,
    local_sem,
    halo_send,
    halo_recv,
    send1,
    recv1,
    send2,
    recv2,
    own_sem,
):
    rows, cols, width_exp = expanded.shape
    width = stream.shape[1]
    half = width // 2
    count = rows * cols
    team = lats * GRID
    stride = lons // GRID
    strip = lats
    head_dim = width // heads
    lat = lax.axis_index("lat")
    lon = lax.axis_index("lon")
    member = lon // stride
    spot = lon % stride
    me = lat * GRID + member

    def where_is(d):
        return {"lat": d // GRID, "lon": (d % GRID) * stride + spot}

    loads = [
        pltpu.make_async_copy(expanded, ext.at[pl.ds(1, rows)], local_sem.at[0]),
        pltpu.make_async_copy(stream, stream_v, local_sem.at[1]),
        pltpu.make_async_copy(w_proj, wp, local_sem.at[2]),
        pltpu.make_async_copy(w_qkv, wq, local_sem.at[3]),
        pltpu.make_async_copy(w_out, wo, local_sem.at[4]),
    ]
    for load in loads:
        load.start()

    north, south = lax.rem(lat + lats - 1, lats), lax.rem(lat + 1, lats)
    west, east = lax.rem(lon + lons - 1, lons), lax.rem(lon + 1, lons)

    barrier = pltpu.get_barrier_semaphore()

    def greet(k, _):
        pl.semaphore_signal(barrier, inc=1, device_id=where_is(lax.rem(me + k, team)))
        return 0

    lax.fori_loop(1, team, greet, 0)
    greeted = team - 1
    if stride > 1:
        for i in (north, lat, south):
            for j in (west, east):
                pl.semaphore_signal(barrier, inc=1, device_id={"lat": i, "lon": j})
        greeted += 6

    loads[0].wait()
    block = ext[1 : rows + 1].reshape(count, width_exp)
    picked = jnp.dot(picks[...], block, preferred_element_type=jnp.float32)
    edges[0] = picked[0:rows].astype(jnp.bfloat16)
    edges[1] = picked[8 : 8 + rows].astype(jnp.bfloat16)
    for c in range(4):
        corners[c] = picked[16 + 8 * c : 17 + 8 * c]
    pl.semaphore_wait(barrier, greeted)

    def halo(src, dst, k, i, j):
        return pltpu.make_async_remote_copy(
            src_ref=src,
            dst_ref=dst,
            send_sem=halo_send.at[k],
            recv_sem=halo_recv.at[k],
            device_id={"lat": i, "lon": j},
        )

    halos = [
        halo(expanded.at[rows - 1], ext.at[0], 0, south, lon),
        halo(expanded.at[0], ext.at[rows + 1], 1, north, lon),
        halo(edges.at[1], side.at[0], 2, lat, east),
        halo(edges.at[0], side.at[1], 3, lat, west),
        halo(corners.at[3], corner_in.at[0], 4, south, east),
        halo(corners.at[2], corner_in.at[1], 5, south, west),
        halo(corners.at[1], corner_in.at[2], 6, north, east),
        halo(corners.at[0], corner_in.at[3], 7, north, west),
    ]
    for copy in halos:
        copy.start()

    lane = lax.broadcasted_iota(jnp.int32, (heads, LANES), 1)
    flat = table[...]
    for n in range(GRID):
        near = flat if n == 0 else pltpu.roll(flat, n, axis=1)
        far = pltpu.roll(flat, LANES - GRID + n, axis=1)
        turned[:, n, :] = jnp.where((lane & (GRID - 1)) >= n, near, far)
    packs = count // (GRID * GRID)
    lane8 = lax.broadcasted_iota(jnp.int32, (GRID, LANES), 1)
    capped = jnp.zeros((GRID, LANES), jnp.int32)
    for m in range(GRID):
        capped = jnp.where(
            (lane8 & (GRID * GRID - 1)) // GRID == m, polar[m * strip + lat], capped
        )
    open_key = capped == 0

    def fill(h, _):
        own = turned[h]
        for g in range(packs):
            lo, hi = g * GRID * GRID, (g + 1) * GRID * GRID
            allowed = open_key & (lane8 >= lo) & (lane8 < hi)
            for m in range(GRID):
                by = (lo + LANES - (GRID - 1 - m) * GRID) % LANES
                moved = own if by == 0 else pltpu.roll(own, by, axis=1)
                at = (g * GRID + m) * GRID
                bias[h, at : at + GRID, :] = jnp.where(allowed, moved, NEVER)
        return 0

    lax.fori_loop(0, heads, fill, 0)

    for copy in halos:
        copy.wait_send()
        copy.wait_recv()

    has_north = jnp.where(lat > 0, 1.0, 0.0)
    has_south = jnp.where(lat < lats - 1, 1.0, 0.0)
    token = lax.broadcasted_iota(jnp.int32, (cols, LANES), 0)

    def filter_lanes(c, _):
        at = pl.ds(pl.multiple_of(c * LANES, LANES), LANES)
        kern = taps[:, at]
        shift_row = shift[:, at]
        west_in = side[0, :, at].astype(jnp.float32)
        east_in = side[1, :, at].astype(jnp.float32)
        shifted = []
        for e in range(rows + 2):
            x = ext[e, :, at].astype(jnp.float32)
            if e == 0:
                x = x * has_north
                lo, hi = corner_in[0, :, at] * has_north, corner_in[1, :, at] * has_north
            elif e == rows + 1:
                x = x * has_south
                lo, hi = corner_in[2, :, at] * has_south, corner_in[3, :, at] * has_south
            else:
                lo, hi = west_in[e - 1 : e], east_in[e - 1 : e]
            before = jnp.where(token == 0, lo, pltpu.roll(x, 1, axis=0))
            after = jnp.where(token == cols - 1, hi, pltpu.roll(x, cols - 1, axis=0))
            shifted.append((before, x, after))
            if e >= 2:
                r = e - 2
                total = land[r] * shift_row
                for a in range(3):
                    for b in range(3):
                        total = total + shifted[r + a][b] * kern[3 * a + b : 3 * a + b + 1]
                act[r * cols : (r + 1) * cols, at] = jax.nn.gelu(total).astype(jnp.bfloat16)
        return 0

    lax.fori_loop(0, width_exp // LANES, filter_lanes, 0)

    loads[1].wait()
    loads[2].wait()
    projected = jnp.dot(act[...], wp[...], preferred_element_type=jnp.float32)
    whole = (stream_v[...].astype(jnp.float32) + projected).astype(jnp.bfloat16)
    whole = whole.astype(jnp.float32)
    mixed[...] = whole
    centred = whole - jnp.mean(whole, axis=1, keepdims=True)
    spread = jnp.mean(centred * centred, axis=1, keepdims=True)
    normed = centred * lax.rsqrt(spread + eps)

    def pack(order, x):
        x = x.astype(jnp.bfloat16)
        stacked = jnp.concatenate([x[:, :half], x[:, half:]], axis=0)
        slabs = jnp.dot(order, stacked, preferred_element_type=jnp.float32)
        return slabs.reshape(team, 2 * count // team, half).astype(jnp.bfloat16)

    def unpack(order_t, slabs):
        flat = slabs.astype(jnp.float32).reshape(2 * count, half).astype(jnp.bfloat16)
        stacked = jnp.dot(order_t, flat, preferred_element_type=jnp.float32)
        return jnp.concatenate([stacked[:count], stacked[count:]], axis=1).astype(jnp.bfloat16)

    def slab(src, dst, sends, recvs, to, at):
        return pltpu.make_async_remote_copy(
            src_ref=src.at[to],
            dst_ref=dst.at[at],
            send_sem=sends.at[to],
            recv_sem=recvs.at[at],
            device_id=where_is(to),
        )

    def exchange(src, dst, sends, recvs, own_at):
        def start(k, _):
            slab(src, dst, sends, recvs, lax.rem(me + k, team), me).start()
            return 0

        def finish(k, _):
            slab(src, dst, sends, recvs, lax.rem(me + k, team), me).wait_send()
            other = lax.rem(me + team - k, team)
            slab(src, dst, sends, recvs, other, other).wait_recv()
            return 0

        own = pltpu.make_async_copy(src.at[me], dst.at[me], own_sem.at[own_at])
        own.start()
        lax.fori_loop(1, team, start, 0)
        own.wait()
        lax.fori_loop(1, team, finish, 0)

    sent1[...] = pack(home[...], normed)
    exchange(sent1, came1, send1, recv1, 0)
    tokens = unpack(away_t[...], came1[...])
    loads[3].wait()
    qkv[...] = jnp.dot(tokens, wq[...], preferred_element_type=jnp.float32).astype(jnp.bfloat16)

    per = LANES // head_dim
    lane_head = lax.broadcasted_iota(jnp.int32, (count, LANES), 1) // head_dim
    scale = head_dim ** (-0.5)
    for p in range(heads // per):
        q = qkv[:, p * LANES : (p + 1) * LANES]
        k = qkv[:, width + p * LANES : width + (p + 1) * LANES]
        v = qkv[:, 2 * width + p * LANES : 2 * width + (p + 1) * LANES]
        zero = jnp.zeros_like(q)
        joined = jnp.zeros((count, LANES), jnp.float32)
        for h in range(per):
            mine = lane_head == h
            scores = lax.dot_general(
                jnp.where(mine, q, zero),
                k,
                (((1,), (1,)), ((), ())),
                preferred_element_type=jnp.float32,
            )
            scores = scores * scale + bias[p * per + h]
            weights = jnp.exp(scores - jnp.max(scores, axis=1, keepdims=True))
            probs = weights / jnp.sum(weights, axis=1, keepdims=True)
            joined = joined + jnp.dot(
                probs.astype(jnp.bfloat16),
                jnp.where(mine, v, zero),
                preferred_element_type=jnp.float32,
            )
        attended[:, p * LANES : (p + 1) * LANES] = joined.astype(jnp.bfloat16)

    sent2[...] = pack(away[...], attended[...])
    exchange(sent2, came2, send2, recv2, 1)
    back = unpack(home_t[...], came2[...])
    loads[4].wait()
    result = mixed[...] + jnp.dot(back, wo[...], preferred_element_type=jnp.float32)
    out[...] = result.astype(jnp.bfloat16)


def local(lats, lons, expanded, stream, land, polar, land_shift, dw_kernel, w_proj, w_qkv, w_out, rel_bias):
    rows, cols, width_exp = expanded.shape
    width = stream.shape[2]
    heads = rel_bias.shape[0]
    count = rows * cols
    team = lats * GRID
    assert rows * lats == GRID * lats and count == LANES and GRID * (2 * GRID - 1) <= LANES
    table = rel_bias.reshape(heads, -1)
    table = jnp.pad(table, ((0, 0), (0, LANES - table.shape[1])))
    home, away = orders(rows, cols, lats)
    bf16, f32 = jnp.bfloat16, jnp.float32
    slabs = (team, 2 * count // team, width // 2)
    any_ = pl.BlockSpec(memory_space=pl.ANY)
    vmem = pl.BlockSpec(memory_space=pltpu.VMEM)
    smem = pl.BlockSpec(memory_space=pltpu.SMEM)
    dma = pltpu.SemaphoreType.DMA
    result = pl.pallas_call(
        functools.partial(kernel, lats, lons, heads),
        out_shape=jax.ShapeDtypeStruct((count, width), bf16),
        in_specs=[any_] * 5 + [smem] + [vmem] * 9,
        out_specs=vmem,
        scratch_shapes=[
            pltpu.VMEM((rows + 2, cols, width_exp), bf16),
            pltpu.VMEM((2, rows, width_exp), bf16),
            pltpu.VMEM((4, 1, width_exp), f32),
            pltpu.VMEM((2, rows, width_exp), bf16),
            pltpu.VMEM((4, 1, width_exp), f32),
            pltpu.VMEM((count, width), bf16),
            pltpu.VMEM(w_proj.shape, bf16),
            pltpu.VMEM(w_qkv.shape, bf16),
            pltpu.VMEM(w_out.shape, bf16),
            pltpu.VMEM((count, width_exp), bf16),
            pltpu.VMEM((count, width), f32),
            pltpu.VMEM((heads, GRID, LANES), f32),
            pltpu.VMEM((heads, count, LANES), f32),
            pltpu.VMEM((count, 3 * width), bf16),
            pltpu.VMEM((count, width), bf16),
            pltpu.VMEM(slabs, bf16),
            pltpu.VMEM(slabs, bf16),
            pltpu.VMEM(slabs, bf16),
            pltpu.VMEM(slabs, bf16),
            dma((5,)),
            dma((8,)),
            dma((8,)),
            dma((team,)),
            dma((team,)),
            dma((team,)),
            dma((team,)),
            dma((2,)),
        ],
        compiler_params=pltpu.CompilerParams(collective_id=0, has_side_effects=True),
        name="section",
    )(
        expanded,
        stream.reshape(count, width),
        w_proj,
        w_qkv,
        w_out,
        polar,
        land.astype(f32)[:, :, None],
        land_shift[None],
        dw_kernel.reshape(9, width_exp),
        table,
        jnp.asarray(edge_picks(rows, cols), bf16),
        jnp.asarray(home, bf16),
        jnp.asarray(home.T, bf16),
        jnp.asarray(away, bf16),
        jnp.asarray(away.T, bf16),
    )
    return result.reshape(rows, cols, width)


def solution(mesh):
    in_specs = (P("lat", "lon", None),) * 2 + (P("lat", "lon"),) + (P(),) * 7
    out_specs = P("lat", "lon", None)
    body = functools.partial(local, mesh.shape["lat"], mesh.shape["lon"])
    return jax.shard_map(body, mesh=mesh, in_specs=in_specs, out_specs=out_specs, check_vma=False)
```

time: 89.3 us -> 44 us (0.49)
  Pallas kernels: 0 us -> 37.5 us
  local copies, waits for them, and re-layouts: 37.1 us -> 5.5 us
  starting transfers between devices: 16.5 us -> 0 us
  matrix products: 14.6 us -> 0 us
  blocking collectives: 13.1 us -> 0 us
  waiting for transfers between devices: 3.82 us -> 0 us
  other arithmetic: 2.62 us -> 0.69 us
    pallas_call x0 -> x1, Pallas kernels: none -> 37.5 us  [local(): pl.pallas_call(functools.partial(kernel, lats, lons, heads), out_shape=ja...]
    all_to_all x1 -> x0, blocking collectives: 13.1 us -> none  [exchange(): lax.all_to_all(x, ('lat', 'lon'), split_axis=0, concat_axis=0, tiled=True)]
    dot_general x5 -> x0, matrix products: 11.8 us -> none  [the longest x1 4.41 us: local(): jnp.dot(activated.reshape(-1, width_exp), w_proj, preferred_element_type=...]
    slice x11 -> x0, local copies, waits for them, and re-layouts: 10.8 us -> none  [the longest x7 6.42 us: full_bias(): jnp.roll(rel_bias, n, axis=2)]
    ppermute x4 -> x0, starting transfers between devices: 9.29 us -> none  [the longest x2 4.9 us: padded(): lax.ppermute(tail, axis, [(i, (i + 1) % count) for i in range(ends)])]
    all_to_all x1 -> x0, starting transfers between devices: 7.24 us -> none  [exchange(): lax.all_to_all(x, ('lat', 'lon'), split_axis=0, concat_axis=0, tiled=True)]
    convert_element_type x2 -> x0, local copies, waits for them, and re-layouts: 4.41 us -> none  [the longest x1 2.29 us: local(): attended = jnp.einsum('ghqk,gkhd->gqhd', probs, qkv[:, :, 2], preferred_e...]
    reshape x6 -> x2, local copies, waits for them, and re-layouts: 6.89 us -> 2.52 us  [the longest x1 1.64 us: local(): dw_kernel.reshape(9, width_exp)]
  transfers between devices with their start and end apart: 5 -> 0, of which waited for: 3 -> 0; matrix products, arithmetic and copies ran while one was open for 17% -> 0% of each run, Pallas kernels for 0% -> 0%
where the time goes in v2:
time: 44 us; the launch traced here: 43.7 us
  Pallas kernels  37.5 us (85%)
  local copies, waits for them, and re-layouts  5.5 us (12%)
  other arithmetic  0.69 us (2%)
    pallas_call x1, Pallas kernels, local(): pl.pallas_call(functools.partial(kernel, lats, lons, heads), out_shape=ja...  37.5 us
    reshape x1, local copies, waits for them, and re-layouts, local(): dw_kernel.reshape(9, width_exp)  1.64 us
    unnamed x1, local copies, waits for them, and re-layouts  1.62 us
    reshape x1, local copies, waits for them, and re-layouts, local(): table = rel_bias.reshape(heads, -1)  0.88 us

profile of v2, /device:TPU:0, one launch (start us, length us, event | category | flops | bytes accessed | tf_op | source)
XLA Modules:
  0.0 43.7 jit_solution(6388519142064246365)
XLA Ops:
  0.0 0.7 %convert_bitcast_fusion = f32[8,16,1]{1,0,2:T(8,128)S(1)} fusion(s32[8,16]{1,0:T(8,128)} %param.17), kind=kLoop, calls=%fused_computation | loop fusion | flops 128 | bytes 1024 | tf_op jit(solution)/shard_map/broadcast_in_dim | solution.py:388
  0.7 0.9 %copy.18 = f32[24,120]{1,0:T(8,128)S(1)} copy(f32[24,120]{0,1:T(8,128)} %bitcast.8) | data formatting | bytes 23040 | tf_op jit(solution)/shard_map/reshape | solution.py:336
  1.6 0.6 %pad.4.table = f32[24,128]{1,0:T(8,128)} pad(f32[24,120]{1,0:T(8,128)S(1)} %copy.18, f32[]{:T(128)} %constant.12.clone.1), padding=0_0x0_8 | pad | bytes 23812 | tf_op jit(solution)/shard_map/jit(_pad)/pad | solution.py:337
  2.2 0.7 %copy.19.land = f32[8,16,1]{2,1,0:T(8,128)} copy(f32[8,16,1]{1,0,2:T(8,128)S(1)} %convert_bitcast_fusion) | data formatting | bytes 1024 | tf_op jit(solution)/shard_map/broadcast_in_dim | solution.py:388
  2.9 1.6 %reshape.13.taps = f32[9,3072]{1,0:T(8,128)} reshape(f32[3,3,3072]{2,1,0:T(4,128)} %param.20) | data formatting | bytes 221184 | tf_op jit(solution)/shard_map/reshape | solution.py:390
  4.6 37.5 %section.1 = bf16[128,768]{1,0:T(8,128)(2,1)} custom-call(bf16[8,16,3072]{2,1,0:T(8,128)(2,1)} %expanded.1, bf16[128,768]{1,0:T(8,128)(2,1)} %bitcast.7, bf16[3072,768]{1,0:T(8,128)(2,1)} %w_proj.1, bf16[768,2304]{1,0:T(8,128)(2,1)} %w_qkv.1, bf16[768,768]{1,0:T(8,128)(2,1)} %w_out.1, s32[32]{0:T(128)} %polar.1, f32[8,16,1]{2,1,0:T(8,128)} %copy.19.land, ...), custom_call_target="tpu_custom_call" | custom-call | tf_op jit(solution)/shard_map/section/pallas_call | solution.py:345
  42.1 1.6 %copy.21 = bf16[8,16,768]{2,1,0:T(8,128)(2,1)} copy(bf16[8,16,768]{2,1,0:T(8,128)(2,1)} %bitcast.6) | data formatting | bytes 393216

commit v3 on v2

--- a/solution.py
+++ b/solution.py
@@ -76,7 +76,10 @@
     wp,
     wq,
     wo,
-    act,
+    partial,
+    total,
+    lands,
+    grid_table,
     mixed,
     turned,
     bias,
@@ -170,34 +173,43 @@
     for copy in halos:
         copy.start()
 
-    lane = lax.broadcasted_iota(jnp.int32, (heads, LANES), 1)
-    flat = table[...]
-    for n in range(GRID):
-        near = flat if n == 0 else pltpu.roll(flat, n, axis=1)
-        far = pltpu.roll(flat, LANES - GRID + n, axis=1)
-        turned[:, n, :] = jnp.where((lane & (GRID - 1)) >= n, near, far)
-    packs = count // (GRID * GRID)
-    lane8 = lax.broadcasted_iota(jnp.int32, (GRID, LANES), 1)
-    capped = jnp.zeros((GRID, LANES), jnp.int32)
-    for m in range(GRID):
-        capped = jnp.where(
-            (lane8 & (GRID * GRID - 1)) // GRID == m, polar[m * strip + lat], capped
-        )
-    open_key = capped == 0
-
-    def fill(h, _):
-        own = turned[h]
-        for g in range(packs):
-            lo, hi = g * GRID * GRID, (g + 1) * GRID * GRID
-            allowed = open_key & (lane8 >= lo) & (lane8 < hi)
-            for m in range(GRID):
-                by = (lo + LANES - (GRID - 1 - m) * GRID) % LANES
-                moved = own if by == 0 else pltpu.roll(own, by, axis=1)
-                at = (g * GRID + m) * GRID
-                bias[h, at : at + GRID, :] = jnp.where(allowed, moved, NEVER)
+    pick = lax.broadcasted_iota(jnp.int32, (cols, cols), 0)
+    eye = (pick == lax.broadcasted_iota(jnp.int32, (cols, cols), 1)).astype(jnp.bfloat16)
+    land_t = lax.dot_general(
+        eye,
+        land[...].astype(jnp.float32).astype(jnp.bfloat16),
+        (((1,), (1,)), ((), ())),
+        preferred_element_type=jnp.float32,
+    )
+    for r in range(rows):
+        lands[r] = jnp.broadcast_to(land_t[:, r : r + 1], (cols, LANES))
+    token = lax.broadcasted_iota(jnp.int32, (cols, LANES), 0)
+
+    def beside(x):
+        before = jnp.where(token == 0, 0.0, pltpu.roll(x, 1, axis=0))
+        after = jnp.where(token == cols - 1, 0.0, pltpu.roll(x, cols - 1, axis=0))
+        return before, x, after
+
+    def filter_own(c, _):
+        at = pl.ds(pl.multiple_of(c * LANES, LANES), LANES)
+        kern = [[taps[a, b : b + 1, at] for b in range(3)] for a in range(3)]
+        shift_row = shift[:, at]
+        near = {}
+        for e in range(1, rows + 2):
+            if e <= rows:
+                near[e] = beside(ext[e, :, at].astype(jnp.float32))
+            r = e - 2
+            if r < 0:
+                continue
+            total_r = lands[r] * shift_row
+            for a in range(3):
+                if r + a in near:
+                    for b in range(3):
+                        total_r = total_r + near[r + a][b] * kern[a][b]
+            partial[r, :, at] = total_r
         return 0
 
-    lax.fori_loop(0, heads, fill, 0)
+    lax.fori_loop(0, width_exp // LANES, filter_own, 0)
 
     for copy in halos:
         copy.wait_send()
@@ -205,42 +217,49 @@
 
     has_north = jnp.where(lat > 0, 1.0, 0.0)
     has_south = jnp.where(lat < lats - 1, 1.0, 0.0)
-    token = lax.broadcasted_iota(jnp.int32, (cols, LANES), 0)
-
-    def filter_lanes(c, _):
-        at = pl.ds(pl.multiple_of(c * LANES, LANES), LANES)
-        kern = taps[:, at]
-        shift_row = shift[:, at]
-        west_in = side[0, :, at].astype(jnp.float32)
-        east_in = side[1, :, at].astype(jnp.float32)
-        shifted = []
-        for e in range(rows + 2):
-            x = ext[e, :, at].astype(jnp.float32)
-            if e == 0:
-                x = x * has_north
-                lo, hi = corner_in[0, :, at] * has_north, corner_in[1, :, at] * has_north
-            elif e == rows + 1:
-                x = x * has_south
-                lo, hi = corner_in[2, :, at] * has_south, corner_in[3, :, at] * has_south
-            else:
-                lo, hi = west_in[e - 1 : e], east_in[e - 1 : e]
-            before = jnp.where(token == 0, lo, pltpu.roll(x, 1, axis=0))
-            after = jnp.where(token == cols - 1, hi, pltpu.roll(x, cols - 1, axis=0))
-            shifted.append((before, x, after))
-            if e >= 2:
-                r = e - 2
-                total = land[r] * shift_row
-                for a in range(3):
+    loads[2].wait()
+    step = 2 * LANES
+    row_of = lax.broadcasted_iota(jnp.int32, (rows, LANES), 0)
+
+    def column(k, at, kern, b):
+        x = side[k, :, at].astype(jnp.float32)
+        above = corner_in[k, :, at] * has_north
+        below = corner_in[2 + k, :, at] * has_south
+        up = jnp.where(row_of == 0, above, pltpu.roll(x, 1, axis=0))
+        down = jnp.where(row_of == rows - 1, below, pltpu.roll(x, rows - 1, axis=0))
+        return up * kern[0][b] + x * kern[1][b] + down * kern[2][b]
+
+    def finish_filter(c, _):
+        pieces = []
+        for block_at in range(2):
+            at = pl.ds(pl.multiple_of(c * step + block_at * LANES, LANES), LANES)
+            kern = [[taps[a, b : b + 1, at] for b in range(3)] for a in range(3)]
+            west_sum = column(0, at, kern, 0)
+            east_sum = column(1, at, kern, 2)
+            done = []
+            for r in range(rows):
+                total_r = partial[r, :, at]
+                if r == 0 or r == rows - 1:
+                    e, a, keep = (0, 0, has_north) if r == 0 else (rows + 1, 2, has_south)
+                    far = beside(ext[e, :, at].astype(jnp.float32) * keep)
                     for b in range(3):
-                        total = total + shifted[r + a][b] * kern[3 * a + b : 3 * a + b + 1]
-                act[r * cols : (r + 1) * cols, at] = jax.nn.gelu(total).astype(jnp.bfloat16)
+                        total_r = total_r + far[b] * kern[a][b]
+                total_r = total_r + jnp.where(token == 0, west_sum[r : r + 1], 0.0)
+                total_r = total_r + jnp.where(token == cols - 1, east_sum[r : r + 1], 0.0)
+                done.append(jax.nn.gelu(total_r).astype(jnp.bfloat16))
+            pieces.append(jnp.concatenate(done, axis=0))
+        weight = wp[pl.ds(pl.multiple_of(c * step, step), step), :]
+        term = jnp.dot(
+            jnp.concatenate(pieces, axis=1), weight, preferred_element_type=jnp.float32
+        )
+        total[...] = total[...] + term
         return 0
 
-    lax.fori_loop(0, width_exp // LANES, filter_lanes, 0)
+    total[...] = jnp.zeros_like(total)
+    lax.fori_loop(0, width_exp // step, finish_filter, 0)
 
     loads[1].wait()
-    loads[2].wait()
-    projected = jnp.dot(act[...], wp[...], preferred_element_type=jnp.float32)
+    projected = total[...]
     whole = (stream_v[...].astype(jnp.float32) + projected).astype(jnp.bfloat16)
     whole = whole.astype(jnp.float32)
     mixed[...] = whole
@@ -268,25 +287,65 @@
             device_id=where_is(to),
         )
 
-    def exchange(src, dst, sends, recvs, own_at):
+    def partner(k, sign):
+        j = (k // lats).astype(jnp.int32)
+        by = GRID // 2 + (2 * (j % 2) - 1) * ((j + 1) // 2)
+        i = (k + 1) % lats
+        return ((lat + lats + sign * i) % lats) * GRID + (member + 2 * GRID + sign * by) % GRID
+
+    def exchange(src, dst, sends, recvs, own_at, meanwhile):
         def start(k, _):
-            slab(src, dst, sends, recvs, lax.rem(me + k, team), me).start()
+            slab(src, dst, sends, recvs, partner(k, 1), me).start()
             return 0
 
         def finish(k, _):
-            slab(src, dst, sends, recvs, lax.rem(me + k, team), me).wait_send()
-            other = lax.rem(me + team - k, team)
+            slab(src, dst, sends, recvs, partner(k, 1), me).wait_send()
+            other = partner(k, -1)
             slab(src, dst, sends, recvs, other, other).wait_recv()
             return 0
 
         own = pltpu.make_async_copy(src.at[me], dst.at[me], own_sem.at[own_at])
         own.start()
-        lax.fori_loop(1, team, start, 0)
+        lax.fori_loop(0, team - 1, start, 0)
+        if meanwhile is not None:
+            meanwhile()
         own.wait()
-        lax.fori_loop(1, team, finish, 0)
+        lax.fori_loop(0, team - 1, finish, 0)
+
+    def spread_bias():
+        lane = lax.broadcasted_iota(jnp.int32, (heads, LANES), 1)
+        grid_table[...] = jnp.zeros_like(grid_table)
+        grid_table[: table.shape[0], :heads] = table[...]
+        flat = grid_table[...].T[:heads]
+        for n in range(GRID):
+            near = flat if n == 0 else pltpu.roll(flat, n, axis=1)
+            far = pltpu.roll(flat, LANES - GRID + n, axis=1)
+            turned[:, n, :] = jnp.where((lane & (GRID - 1)) >= n, near, far)
+        packs = count // (GRID * GRID)
+        lane8 = lax.broadcasted_iota(jnp.int32, (GRID, LANES), 1)
+        capped = jnp.zeros((GRID, LANES), jnp.int32)
+        for m in range(GRID):
+            capped = jnp.where(
+                (lane8 & (GRID * GRID - 1)) // GRID == m, polar[m * strip + lat], capped
+            )
+        open_key = capped == 0
+
+        def fill(h, _):
+            own = turned[h]
+            for g in range(packs):
+                lo, hi = g * GRID * GRID, (g + 1) * GRID * GRID
+                allowed = open_key & (lane8 >= lo) & (lane8 < hi)
+                for m in range(GRID):
+                    by = (lo + LANES - (GRID - 1 - m) * GRID) % LANES
+                    moved = own if by == 0 else pltpu.roll(own, by, axis=1)
+                    at = (g * GRID + m) * GRID
+                    bias[h, at : at + GRID, :] = jnp.where(allowed, moved, NEVER)
+            return 0
+
+        lax.fori_loop(0, heads, fill, 0)
 
     sent1[...] = pack(home[...], normed)
-    exchange(sent1, came1, send1, recv1, 0)
+    exchange(sent1, came1, send1, recv1, 0, spread_bias)
     tokens = unpack(away_t[...], came1[...])
     loads[3].wait()
     qkv[...] = jnp.dot(tokens, wq[...], preferred_element_type=jnp.float32).astype(jnp.bfloat16)
@@ -319,7 +378,7 @@
         attended[:, p * LANES : (p + 1) * LANES] = joined.astype(jnp.bfloat16)
 
     sent2[...] = pack(away[...], attended[...])
-    exchange(sent2, came2, send2, recv2, 1)
+    exchange(sent2, came2, send2, recv2, 1, None)
     back = unpack(home_t[...], came2[...])
     loads[4].wait()
     result = mixed[...] + jnp.dot(back, wo[...], preferred_element_type=jnp.float32)
@@ -333,8 +392,7 @@
     count = rows * cols
     team = lats * GRID
     assert rows * lats == GRID * lats and count == LANES and GRID * (2 * GRID - 1) <= LANES
-    table = rel_bias.reshape(heads, -1)
-    table = jnp.pad(table, ((0, 0), (0, LANES - table.shape[1])))
+    table = jnp.transpose(rel_bias, (1, 2, 0)).reshape(-1, heads)
     home, away = orders(rows, cols, lats)
     bf16, f32 = jnp.bfloat16, jnp.float32
     slabs = (team, 2 * count // team, width // 2)
@@ -357,7 +415,10 @@
             pltpu.VMEM(w_proj.shape, bf16),
             pltpu.VMEM(w_qkv.shape, bf16),
             pltpu.VMEM(w_out.shape, bf16),
-            pltpu.VMEM((count, width_exp), bf16),
+            pltpu.VMEM((rows, cols, width_exp), f32),
+            pltpu.VMEM((count, width), f32),
+            pltpu.VMEM((rows, cols, LANES), f32),
+            pltpu.VMEM((LANES, LANES), f32),
             pltpu.VMEM((count, width), f32),
             pltpu.VMEM((heads, GRID, LANES), f32),
             pltpu.VMEM((heads, count, LANES), f32),
@@ -385,9 +446,9 @@
         w_qkv,
         w_out,
         polar,
-        land.astype(f32)[:, :, None],
+        land,
         land_shift[None],
-        dw_kernel.reshape(9, width_exp),
+        dw_kernel,
         table,
         jnp.asarray(edge_picks(rows, cols), bf16),
         jnp.asarray(home, bf16),

time: 44 us -> 39.1 us (0.89)
  local copies, waits for them, and re-layouts: 5.5 us -> 1.62 us
  other arithmetic: 0.69 us -> 0 us
    reshape x2 -> x0, local copies, waits for them, and re-layouts: 2.52 us -> none  [the longest x1 1.64 us: local(): dw_kernel.reshape(9, width_exp)]
    broadcast_in_dim x1 -> x0, local copies, waits for them, and re-layouts: 0.74 us -> none  [local(): land.astype(f32)[:, :, None]]
    broadcast_in_dim x1 -> x0, other arithmetic: 0.69 us -> none  [local(): land.astype(f32)[:, :, None]]
    pad x1 -> x0, local copies, waits for them, and re-layouts: 0.62 us -> none  [local(): table = jnp.pad(table, ((0, 0), (0, LANES - table.shape[1])))]
where the time goes in v3:
time: 39.1 us; the launch traced here: 38.8 us
  Pallas kernels  37.2 us (95%)
  local copies, waits for them, and re-layouts  1.62 us (4%)
    pallas_call x1, Pallas kernels, local(): pl.pallas_call(functools.partial(kernel, lats, lons, heads), out_shape=ja...  37.2 us
    unnamed x1, local copies, waits for them, and re-layouts  1.62 us

profile of v3, /device:TPU:0, one launch (start us, length us, event | category | flops | bytes accessed | tf_op | source)
XLA Modules:
  0.0 38.8 jit_solution(7548343963357979308)
XLA Ops:
  0.0 37.2 %section.1 = bf16[128,768]{1,0:T(8,128)(2,1)} custom-call(bf16[8,16,3072]{2,1,0:T(8,128)(2,1)} %expanded.1, bf16[128,768]{1,0:T(8,128)(2,1)} %bitcast.7, bf16[3072,768]{1,0:T(8,128)(2,1)} %w_proj.1, bf16[768,2304]{1,0:T(8,128)(2,1)} %w_qkv.1, bf16[768,768]{1,0:T(8,128)(2,1)} %w_out.1, s32[32]{0:T(128)} %polar.1, s32[8,16]{1,0:T(8,128)} %land.1, ...), custom_call_target="tpu_custom_call" | custom-call | tf_op jit(solution)/shard_map/section/pallas_call | solution.py:403
  37.2 1.6 %copy.17 = bf16[8,16,768]{2,1,0:T(8,128)(2,1)} copy(bf16[8,16,768]{2,1,0:T(8,128)(2,1)} %bitcast.6) | data formatting | bytes 393216

commit v4 on v3

--- a/solution.py
+++ b/solution.py
@@ -62,10 +62,10 @@
     taps,
     table,
     picks,
-    home,
-    home_t,
-    away,
-    away_t,
+    home_in,
+    home_t_in,
+    away_in,
+    away_t_in,
     out,
     ext,
     edges,
@@ -89,6 +89,7 @@
     came1,
     sent2,
     came2,
+    order_v,
     local_sem,
     halo_send,
     halo_recv,
@@ -122,6 +123,8 @@
         pltpu.make_async_copy(w_qkv, wq, local_sem.at[3]),
         pltpu.make_async_copy(w_out, wo, local_sem.at[4]),
     ]
+    for k, order in enumerate((home_in, away_t_in, away_in, home_t_in)):
+        loads.append(pltpu.make_async_copy(order, order_v.at[k], local_sem.at[5 + k]))
     for load in loads:
         load.start()
 
@@ -344,9 +347,11 @@
 
         lax.fori_loop(0, heads, fill, 0)
 
-    sent1[...] = pack(home[...], normed)
+    for load in loads[5:]:
+        load.wait()
+    sent1[...] = pack(order_v[0], normed)
     exchange(sent1, came1, send1, recv1, 0, spread_bias)
-    tokens = unpack(away_t[...], came1[...])
+    tokens = unpack(order_v[1], came1[...])
     loads[3].wait()
     qkv[...] = jnp.dot(tokens, wq[...], preferred_element_type=jnp.float32).astype(jnp.bfloat16)
 
@@ -377,9 +382,9 @@
             )
         attended[:, p * LANES : (p + 1) * LANES] = joined.astype(jnp.bfloat16)
 
-    sent2[...] = pack(away[...], attended[...])
+    sent2[...] = pack(order_v[2], attended[...])
     exchange(sent2, came2, send2, recv2, 1, None)
-    back = unpack(home_t[...], came2[...])
+    back = unpack(order_v[3], came2[...])
     loads[4].wait()
     result = mixed[...] + jnp.dot(back, wo[...], preferred_element_type=jnp.float32)
     out[...] = result.astype(jnp.bfloat16)
@@ -403,7 +408,7 @@
     result = pl.pallas_call(
         functools.partial(kernel, lats, lons, heads),
         out_shape=jax.ShapeDtypeStruct((count, width), bf16),
-        in_specs=[any_] * 5 + [smem] + [vmem] * 9,
+        in_specs=[any_] * 5 + [smem] + [vmem] * 5 + [any_] * 4,
         out_specs=vmem,
         scratch_shapes=[
             pltpu.VMEM((rows + 2, cols, width_exp), bf16),
@@ -428,7 +433,8 @@
             pltpu.VMEM(slabs, bf16),
             pltpu.VMEM(slabs, bf16),
             pltpu.VMEM(slabs, bf16),
-            dma((5,)),
+            pltpu.VMEM((4,) + home.shape, bf16),
+            dma((9,)),
             dma((8,)),
             dma((8,)),
             dma((team,)),

time: 39.1 us -> 38.8 us (level)
  no operation moved by 1% of the time
where the time goes in v4:
time: 38.8 us; the launch traced here: 38.6 us
  Pallas kernels  37 us (95%)
  local copies, waits for them, and re-layouts  1.62 us (4%)
    pallas_call x1, Pallas kernels, local(): pl.pallas_call(functools.partial(kernel, lats, lons, heads), out_shape=ja...  37 us
    unnamed x1, local copies, waits for them, and re-layouts  1.62 us

profile of v4, /device:TPU:0, one launch (start us, length us, event | category | flops | bytes accessed | tf_op | source)
XLA Modules:
  0.0 38.6 jit_solution(354264012346507427)
XLA Ops:
  0.0 37.0 %section.1 = bf16[128,768]{1,0:T(8,128)(2,1)} custom-call(bf16[8,16,3072]{2,1,0:T(8,128)(2,1)} %expanded.1, bf16[128,768]{1,0:T(8,128)(2,1)} %bitcast.7, bf16[3072,768]{1,0:T(8,128)(2,1)} %w_proj.1, bf16[768,2304]{1,0:T(8,128)(2,1)} %w_qkv.1, bf16[768,768]{1,0:T(8,128)(2,1)} %w_out.1, s32[32]{0:T(128)} %polar.1, s32[8,16]{1,0:T(8,128)} %land.1, ...), custom_call_target="tpu_custom_call" | custom-call | tf_op jit(solution)/shard_map/section/pallas_call | solution.py:408
  37.0 1.6 %copy.17 = bf16[8,16,768]{2,1,0:T(8,128)(2,1)} copy(bf16[8,16,768]{2,1,0:T(8,128)(2,1)} %bitcast.6) | data formatting | bytes 393216
